TPU v7x, 256 devices: a whole 4x4x8 slice. The times are simulated.
256 devices in a mesh: head: 8 (over z_lo, core), blk: 32 (over y, x, z_hi).
Axes of the slice: x: 4, y: 4, z: 8 (z_hi: 2, z_lo: 4; z = z_hi * 4 + z_lo), core: 2. Of those that a mesh axis runs over, the one named last changes fastest.
Arguments:
- query_act: bfloat16 [8192, 5120], P(('blk', 'head')), may hold values from -6 to 6
- key_act: bfloat16 [8192, 1024], P(('blk', 'head')), may hold values from -6 to 6
- value_act: bfloat16 [8192, 1024], P(('blk', 'head')), may hold values from -6 to 6
- attn_out: bfloat16 [8192, 5120], P(('blk', 'head')), may hold values from -4 to 4
- grad_out: bfloat16 [8192, 5120], P(('blk', 'head')), may hold values from -6 to 6
- log_sum: float32 [8192, 40], P(('blk', 'head')), may hold values from 5 to 6.5
- kv_lists: int32 [64, 32], P('blk'), may hold values from -1 to 63, as said below
Outputs:
- grad_query: bfloat16 [8192, 5120], P(('blk', 'head'))
- grad_key: bfloat16 [8192, 1024], P(('blk', 'head'))
- grad_value: bfloat16 [8192, 1024], P(('blk', 'head'))
Inputs may be any that keep to these rules, and one draw needn't show every extreme that they name: `kv_lists`: the pack is made of prompt trees: the first holds 16 blocks, the last 16, and those between 32 blocks each, in order. A tree is a prompt, then branches. Row r names in rising order the blocks whose keys block r sees (the tree's prompt blocks up to r, and the earlier blocks of r's branch), then -1 to the end. Every entry lies in the same tree as r and is at most r; r itself is always named.
All inputs are finite; a program needn't handle non-finite values.
Results may differ from a plain program's by a relative error of at most 0.0049.
Values may be sent and summed in bfloat16 or wider, within the bound.
A program may use at most 64 MiB of HBM per device.

v0:
```python
import jax
import jax.numpy as jnp
from jax import lax
from jax.experimental import pallas as pl
from jax.experimental.pallas import tpu as pltpu
from jax.sharding import PartitionSpec as P

QH = 40
KVH = 8
HD = 128
BLOCK = 128
GS = QH // KVH
TOK = 32
GW = GS * HD
PIECE = 64
ROWS = GS * PIECE
NX = 4
NZ = 8
PEERS = 8
LISTW = 32
SCALE = HD ** -0.5
LOG2E = 1.4426950408889634
MESH = pl.DeviceIdType.MESH
F32 = jnp.float32
BF16 = jnp.bfloat16
NT = (((1,), (1,)), ((), ()))
NN = (((1,), (0,)), ((), ()))


def coords():
    blk = lax.axis_index("blk")
    head = lax.axis_index("head")
    y = blk // 8
    x = (blk // 2) % 4
    z = (blk % 2) * 4 + head // 2
    return y, x, z, head % 2


def device(y, x, z, core):
    return {"blk": (y * 4 + x) * 2 + z // 4, "head": (z % 4) * 2 + core}


def remote(src, dst, send_sem, recv_sem, device_id):
    return pltpu.make_async_remote_copy(
        src_ref=src,
        dst_ref=dst,
        send_sem=send_sem,
        recv_sem=recv_sem,
        device_id=device_id,
        device_id_type=MESH,
    )


def signal_peers(bar, y, x, z, core, me):
    for d in range(1, PEERS):
        p = (me + d) % PEERS
        pl.semaphore_signal(bar, inc=1, device_id=device(y, p // 2, z, p % 2), device_id_type=MESH)
    for step in (1, NZ - 1):
        pl.semaphore_signal(
            bar, inc=1, device_id=device(y, x, (z + step) % NZ, core), device_id_type=MESH
        )

    @pl.when((y == 1) | (y == 2))
    def _():
        pl.semaphore_signal(bar, inc=1, device_id=device(3 - y, x, z, core), device_id_type=MESH)


def wait_peers(bar, y):
    pl.semaphore_wait(bar, PEERS - 1 + 2 + ((y == 1) | (y == 2)).astype(jnp.int32))


CHAINS = ((0, 0, 4), (0, 1, 3), (1, 1, 4), (1, 0, 3))


NEAR = ((0, 1), (1, 0), (3, 0), (1, 1), (3, 1), (2, 0), (2, 1))


def gather_kernel(
    q, k, v, o, do, lse, lists,
    qg, dog, stg, lsg, kvg,
    o_buf, do_buf, lse_buf, rows_buf, stat_src, list_src, in_sem,
    kv_s, kv_r, kv_l, big_s, big_r, big_l, st_s, st_r, st_l, ls_s, ls_r, ls_l,
    ring_s, ring_r, cr_s, cr_r, crst_s, crst_r, crls_s, crls_r,
):
    y, x, z, core = coords()
    me = x * 2 + core
    loads = [
        pltpu.make_async_copy(src, dst, in_sem.at[i])
        for i, (src, dst) in enumerate(
            ((lists, rows_buf), (lse, lse_buf), (do, do_buf), (o, o_buf))
        )
    ]
    for c in loads:
        c.start()
    bar = pltpu.get_barrier_semaphore()
    signal_peers(bar, y, x, z, core, me)

    def cols(ref, g, width):
        return ref.at[:, pl.ds(pl.multiple_of(g * width, 128), width)]

    def to(n):
        return ((x + n[0]) % NX) * 2 + (core + n[1]) % 2

    def of(n):
        return ((x + NX - n[0]) % NX) * 2 + (core + n[1]) % 2

    def at(p):
        return device(y, p // 2, z, p % 2)

    def kv_slot(s, piece, zz):
        return kvg.at[zz, piece, s // 2, pl.ds((s % 2) * TOK, TOK), :]

    def kv_copy(p, piece):
        return remote(
            cols((k, v)[piece], p, HD), kv_slot(me, piece, z),
            kv_s.at[piece, p], kv_r.at[piece, me], at(p),
        )

    def kv_recv(s, piece):
        return remote(
            cols((k, v)[piece], s, HD), kv_slot(s, piece, z),
            kv_s.at[piece, s], kv_r.at[piece, s], at(s),
        )

    def big_copy(p, which):
        src, dst = ((q, qg), (do, dog))[which]
        return remote(
            cols(src, p, GW), dst.at[0, me], big_s.at[which, p], big_r.at[which, me], at(p)
        )

    def big_recv(s, which):
        src, dst = ((q, qg), (do, dog))[which]
        return remote(
            cols(src, s, GW), dst.at[0, s], big_s.at[which, s], big_r.at[which, s], at(s)
        )

    def st_copy(p):
        return remote(stat_src.at[p], stg.at[0, me], st_s.at[p], st_r.at[me], at(p))

    def st_recv(s):
        return remote(stat_src.at[s], stg.at[0, s], st_s.at[s], st_r.at[s], at(s))

    def ls_copy(d):
        xx = (x + d) % NX
        return remote(list_src, lsg.at[0, x], ls_s.at[xx], ls_r.at[x], device(y, xx, z, core))

    def ls_recv(d):
        xx = (x + NX - d) % NX
        return remote(list_src, lsg.at[0, xx], ls_s.at[xx], ls_r.at[xx], device(y, xx, z, core))

    def cross_copy(s, which):
        ref = (qg, dog)[which]
        return remote(
            ref.at[0, s], ref.at[1, s], cr_s.at[which, s], cr_r.at[which, s],
            device(3 - y, x, z, core),
        )

    kv_local = [
        pltpu.make_async_copy(cols((k, v)[piece], me, HD), kv_slot(me, piece, z), kv_l.at[piece])
        for piece in (0, 1)
    ]
    big_local = [
        pltpu.make_async_copy(cols(q, me, GW), qg.at[0, me], big_l.at[0]),
        pltpu.make_async_copy(cols(do, me, GW), dog.at[0, me], big_l.at[1]),
    ]
    for c in kv_local + big_local:
        c.start()

    loads[0].wait()
    rows = rows_buf[...]
    count = jnp.sum(jnp.where(rows >= 0, 1.0, 0.0), axis=1, keepdims=True).astype(jnp.int32)
    early = jnp.sum(
        jnp.where((rows >= 0) & (rows < 32), 1.0, 0.0), axis=1, keepdims=True
    ).astype(jnp.int32)
    list_src[...] = jnp.zeros((8, 128), jnp.int32)
    list_src[0:2, 0:LISTW] = rows
    lane = lax.broadcasted_iota(jnp.int32, (2, 128), 1)
    list_src[4:6, :] = jnp.where(lane == 0, count, early)

    for c in loads[1:]:
        c.wait()
    lane = lax.broadcasted_iota(jnp.int32, (TOK, 128), 1)
    for g in range(KVH):
        block = jnp.zeros((TOK, 128), F32)
        for r in range(GS):
            h = g * GS + r
            own = slice(h * HD, (h + 1) * HD)
            delta = jnp.sum(
                do_buf[:, own].astype(F32) * o_buf[:, own].astype(F32), axis=1, keepdims=True
            )
            block = jnp.where(lane == r, lse_buf[:, h : h + 1] * LOG2E, block)
            block = jnp.where(lane == 8 + r, delta, block)
        stat_src[g] = block

    wait_peers(bar, y)
    for piece in (0, 1):
        for n in NEAR[1:] + NEAR[:1]:
            kv_copy(to(n), piece).start()
    for n in NEAR:
        for which in (0, 1):
            big_copy(to(n), which).start()
    for c in big_local:
        c.wait()

    @pl.when(y == 2)
    def _():
        for which in (0, 1):
            cross_copy(me, which).start()

    for n in NEAR:
        st_copy(to(n)).start()
    for d in range(1, NX):
        ls_copy(d).start()
    st_local = pltpu.make_async_copy(stat_src.at[me], stg.at[0, me], st_l)
    st_local.start()
    ls_local = pltpu.make_async_copy(list_src, lsg.at[0, x], ls_l)
    ls_local.start()

    def ring_copy(direction, piece, step):
        sign = (1, NZ - 1)[direction]
        back = (NZ - 1, 1)[direction]
        chunk = (z + back * step) % NZ
        part = kvg.at[chunk, piece]
        return remote(
            part, part, ring_s.at[direction, piece, step], ring_r.at[direction, piece, step],
            device(y, x, (z + sign) % NZ, core),
        )

    def ring_recv(direction, piece, step):
        back = (NZ - 1, 1)[direction]
        chunk = (z + back * (step + 1)) % NZ
        part = kvg.at[chunk, piece]
        return remote(
            part, part, ring_s.at[direction, piece, step], ring_r.at[direction, piece, step],
            device(y, x, (z + back) % NZ, core),
        )

    def forward(some):
        for n in some:
            s = of(n)
            for which in (0, 1):
                big_recv(s, which).wait_recv()

            @pl.when(y == 2)
            def _():
                for which in (0, 1):
                    cross_copy(s, which).start()

    def ring_start(piece):
        for n in NEAR:
            kv_recv(of(n), piece).wait_recv()
        kv_local[piece].wait()
        for direction in (0, 1):
            ring_copy(direction, piece, 0).start()

    def ring_step(step, piece):
        for direction, pc, steps in CHAINS:
            if pc == piece and step < steps:
                ring_recv(direction, piece, step).wait_recv()
                if step + 1 < steps:
                    ring_copy(direction, piece, step + 1).start()

    ring_start(0)
    ring_start(1)
    forward(NEAR[:3])
    ring_step(0, 0)
    forward(NEAR[3:4])
    ring_step(0, 1)
    forward(NEAR[4:5])
    ring_step(1, 0)
    forward(NEAR[5:6])
    ring_step(1, 1)
    forward(NEAR[6:])

    for n in NEAR:
        st_recv(of(n)).wait_recv()
    for d in range(1, NX):
        ls_recv(d).wait_recv()
    st_local.wait()
    ls_local.wait()

    crst = remote(stg.at[0], stg.at[1], crst_s, crst_r, device(3 - y, x, z, core))
    crls = remote(lsg.at[0], lsg.at[1], crls_s, crls_r, device(3 - y, x, z, core))

    @pl.when(y == 2)
    def _():
        crst.start()
        crls.start()

    for step in (2, 3):
        for piece in (0, 1):
            ring_step(step, piece)

    for n in NEAR:
        for i in (0, 1):
            kv_copy(to(n), i).wait_send()
            big_copy(to(n), i).wait_send()
        st_copy(to(n)).wait_send()
    for d in range(1, NX):
        ls_copy(d).wait_send()
    for direction, piece, steps in CHAINS:
        for step in range(steps):
            ring_copy(direction, piece, step).wait_send()

    @pl.when(y == 2)
    def _():
        for s in range(PEERS):
            for which in (0, 1):
                cross_copy(s, which).wait_send()
        crst.wait_send()
        crls.wait_send()

    @pl.when(y == 1)
    def _():
        for s in range(PEERS):
            for which in (0, 1):
                cross_copy(s, which).wait_recv()
        crst.wait_recv()
        crls.wait_recv()


def gather(q, k, v, o, do, lse, lists):
    vmem = pl.BlockSpec(memory_space=pltpu.VMEM)
    hbm = pl.BlockSpec(memory_space=pltpu.HBM)
    dma = pltpu.SemaphoreType.DMA
    return pl.pallas_call(
        gather_kernel,
        out_shape=(
            jax.ShapeDtypeStruct((2, PEERS, TOK, GW), BF16),
            jax.ShapeDtypeStruct((2, PEERS, TOK, GW), BF16),
            jax.ShapeDtypeStruct((2, PEERS, TOK, 128), F32),
            jax.ShapeDtypeStruct((2, NX, 8, 128), jnp.int32),
            jax.ShapeDtypeStruct((NZ, 2, NX, PIECE, HD), BF16),
        ),
        in_specs=[hbm] * 7,
        out_specs=(vmem,) * 5,
        scratch_shapes=[
            pltpu.VMEM((TOK, QH * HD), BF16),
            pltpu.VMEM((TOK, QH * HD), BF16),
            pltpu.VMEM((TOK, QH), F32),
            pltpu.VMEM((2, LISTW), jnp.int32),
            pltpu.VMEM((KVH, TOK, 128), F32),
            pltpu.VMEM((8, 128), jnp.int32),
            dma((4,)),
            dma((2, PEERS)), dma((2, PEERS)), dma((2,)),
            dma((2, PEERS)), dma((2, PEERS)), dma((2,)),
            dma((PEERS,)), dma((PEERS,)), dma,
            dma((NX,)), dma((NX,)), dma,
            dma((2, 2, 4)), dma((2, 2, 4)),
            dma((2, PEERS)), dma((2, PEERS)),
            dma, dma, dma, dma,
        ],
        compiler_params=pltpu.CompilerParams(
            collective_id=0, has_side_effects=True, vmem_limit_bytes=16 << 20
        ),
        name="gather",
    )(q, k, v, o, do, lse, lists)


def attend_kernel(
    lists, qg, dog, stg, kvg, dq, dkv,
    qs, dos, qt, dot, lseb, delb, dqa, dka, dva,
):
    y, x, z, core = coords()
    half = (z % 4) // 2
    base = y * 16
    for ref in (dka, dva):
        ref[...] = jnp.zeros_like(ref)
    r_id = lax.broadcasted_iota(jnp.int32, (128, 128), 0)
    c_id = lax.broadcasted_iota(jnp.int32, (128, 128), 1)
    eye = jnp.where(r_id == c_id, 1.0, 0.0).astype(BF16)
    row_tok = (z % 2) * PIECE + lax.broadcasted_iota(jnp.int32, (ROWS, 128), 0) % PIECE
    key_tok = lax.broadcasted_iota(jnp.int32, (ROWS, 128), 1)

    def chunk(i, carry):
        part = i // NX
        xx = i % NX
        total = lists[part, xx, 4 + half, 0]
        early = lists[part, xx, 4 + half, 1]
        own = part == 0
        lo = jnp.where(own & (y == 2), early, 0)
        hi = jnp.where(own, total, jnp.where(y == 1, early, 0))
        n = hi - lo
        diag = jnp.where(own, xx * 4 + z // 2, -1)

        @pl.when(n > 0)
        def _():
            for c in range(2):
                st = stg[part, xx * 2 + c]
                for r in range(GS):
                    at = slice(r * PIECE + c * TOK, r * PIECE + (c + 1) * TOK)
                    col = slice(r * HD, (r + 1) * HD)
                    qs[at, :] = qg[part, xx * 2 + c, :, col]
                    dos[at, :] = dog[part, xx * 2 + c, :, col]
                    lseb[at, :] = jnp.broadcast_to(st[:, r : r + 1], (TOK, 128))
                    delb[at, :] = jnp.broadcast_to(st[:, 8 + r : 9 + r], (TOK, 128))
            qt[...] = lax.dot_general(eye, qs[...], NT, preferred_element_type=F32).astype(BF16)
            dot[...] = lax.dot_general(eye, dos[...], NT, preferred_element_type=F32).astype(BF16)
            dqa[...] = jnp.zeros_like(dqa)

            def block(piece, b):
                zz = (b % 4) * 2
                return jnp.concatenate(
                    [kvg[zz, piece, b // 4], kvg[zz + 1, piece, b // 4]], axis=0
                )

            def pair(j, masked):
                a = lists[part, xx, half, j] - base
                if masked:
                    has = j + 1 < hi
                    b = jnp.where(has, lists[part, xx, half, jnp.where(has, j + 1, j)] - base, a)
                else:
                    b = lists[part, xx, half, j + 1] - base
                keys = jnp.concatenate([block(0, a), block(0, b)], axis=0)
                values = jnp.concatenate([block(1, a), block(1, b)], axis=0)
                s = lax.dot_general(qs[...], keys, NT, preferred_element_type=F32)
                lse2 = jnp.concatenate([lseb[...], lseb[...]], axis=1)
                del2 = jnp.concatenate([delb[...], delb[...]], axis=1)
                p = jnp.exp2(s * (SCALE * LOG2E) - lse2)
                if masked:
                    ta = row_tok + jnp.where(a == diag, 0, BLOCK)
                    tb = row_tok + jnp.where(has, jnp.where(b == diag, 0, BLOCK), -2 * BLOCK)
                    seen = jnp.concatenate([key_tok <= ta, key_tok <= tb], axis=1)
                    p = jnp.where(seen, p, 0.0)
                dp = lax.dot_general(dos[...], values, NT, preferred_element_type=F32)
                ds = (p * (dp - del2)).astype(BF16)
                pb = p.astype(BF16)
                dvt = lax.dot_general(dot[...], pb, NN, preferred_element_type=F32)
                dkt = lax.dot_general(qt[...], ds, NN, preferred_element_type=F32)
                dqa[...] += lax.dot_general(ds, keys, NN, preferred_element_type=F32)
                dva[a] += dvt[:, :BLOCK]
                dka[a] += dkt[:, :BLOCK]
                dva[b] += dvt[:, BLOCK:]
                dka[b] += dkt[:, BLOCK:]

            full = (n - 1) // 2

            def step(t, carry):
                pair(lo + 2 * t, False)
                return carry

            lax.fori_loop(0, full, step, 0)
            pair(lo + 2 * full, True)
            for c in range(2):
                for r in range(GS):
                    at = slice(r * PIECE + c * TOK, r * PIECE + (c + 1) * TOK)
                    col = slice(r * HD, (r + 1) * HD)
                    dq[part, xx * 2 + c, :, col] = (dqa[at, :] * SCALE).astype(BF16)

        @pl.when((n <= 0) & (y == 1))
        def _():
            for c in range(2):
                dq[part, xx * 2 + c] = jnp.zeros((TOK, GW), BF16)

        return carry

    lax.fori_loop(0, jnp.where(y == 1, 2 * NX, NX), chunk, 0)

    def finish(b, carry):
        zz = (b % 4) * 2
        for piece, ref, scale in ((0, dka, SCALE), (1, dva, 1.0)):
            low = (ref[b] * scale).astype(BF16)
            out = lax.dot_general(eye, low, NT, preferred_element_type=F32).astype(BF16)
            dkv[zz, piece, b // 4] = out[:PIECE]
            dkv[zz + 1, piece, b // 4] = out[PIECE:]
        return carry

    lax.fori_loop(0, 16, finish, 0)


def attend(lists, qg, dog, stg, kvg):
    vmem = pl.BlockSpec(memory_space=pltpu.VMEM)
    return pl.pallas_call(
        attend_kernel,
        out_shape=(
            jax.ShapeDtypeStruct((2, PEERS, TOK, GW), BF16),
            jax.ShapeDtypeStruct((NZ, 2, NX, PIECE, HD), BF16),
        ),
        in_specs=[pl.BlockSpec(memory_space=pltpu.SMEM)] + [vmem] * 4,
        out_specs=(vmem, vmem),
        scratch_shapes=[
            pltpu.VMEM((ROWS, HD), BF16),
            pltpu.VMEM((ROWS, HD), BF16),
            pltpu.VMEM((HD, ROWS), BF16),
            pltpu.VMEM((HD, ROWS), BF16),
            pltpu.VMEM((ROWS, 128), F32),
            pltpu.VMEM((ROWS, 128), F32),
            pltpu.VMEM((ROWS, HD), F32),
            pltpu.VMEM((16, HD, BLOCK), F32),
            pltpu.VMEM((16, HD, BLOCK), F32),
        ],
        compiler_params=pltpu.CompilerParams(vmem_limit_bytes=16 << 20),
        name="attend",
    )(lists, qg, dog, stg, kvg)


def give_kernel(
    dq, dkv, gq, gk, gv,
    land, total, acc_in, acc_out, final,
    cr_s, cr_r, ring_s, ring_r, q_s, q_r, q_l, kv_s, kv_r, kv_l,
):
    y, x, z, core = coords()
    me = x * 2 + core
    bar = pltpu.get_barrier_semaphore()
    signal_peers(bar, y, x, z, core, me)
    wait_peers(bar, y)

    def cols(ref, g, width):
        return ref.at[:, pl.ds(pl.multiple_of(g * width, 128), width)]

    def cross_copy(s):
        return remote(dq.at[1, s], land.at[s], cr_s.at[s], cr_r.at[s], device(3 - y, x, z, core))

    slots = [(me + d) % PEERS for d in (2, 3, 4, 5, 6, 7, 1, 0)]

    @pl.when(y == 1)
    def _():
        for s in slots:
            cross_copy(s).start()

    def ring_copy(direction, piece, steps, step):
        sign = (1, NZ - 1)[direction]
        owner = (z + sign * (steps - step)) % NZ
        if step == 0:
            src = dkv.at[owner, piece]
        else:
            src = acc_out.at[direction, piece, step]
        return remote(
            src, acc_in.at[direction, piece, step],
            ring_s.at[direction, piece, step], ring_r.at[direction, piece, step],
            device(y, x, (z + sign) % NZ, core),
        )

    for direction, piece, steps in CHAINS:
        ring_copy(direction, piece, steps, 0).start()

    def q_copy(src, p):
        return remote(
            src.at[p], cols(gq, me, GW), q_s.at[p], q_r.at[me], device(y, p // 2, z, p % 2)
        )

    def q_recv(s):
        return remote(
            total.at[s], cols(gq, s, GW), q_s.at[s], q_r.at[s], device(y, s // 2, z, s % 2)
        )

    q_local = pltpu.make_async_copy(total.at[me], cols(gq, me, GW), q_l)
    q_local_direct = pltpu.make_async_copy(dq.at[0, me], cols(gq, me, GW), q_l)

    @pl.when(y != 2)
    def _():
        for p in slots[:-1]:
            q_copy(dq.at[0], p).start()
        q_local_direct.start()

    def add_cross(some):
        @pl.when(y == 2)
        def _():
            for s in some:
                cross_copy(s).wait_recv()
                total[s] = (dq[0, s].astype(F32) + land[s].astype(F32)).astype(BF16)
                if s is slots[-1]:
                    q_local.start()
                else:
                    q_copy(total, s).start()

    groups = ((), slots[0:2], slots[2:5], slots[5:8])
    for step in range(1, 4):
        for direction, piece, steps in CHAINS:
            if step < steps:
                sign = (1, NZ - 1)[direction]
                owner = (z + sign * (steps - step)) % NZ
                ring_copy(direction, piece, steps, step - 1).wait_recv()
                acc_out[direction, piece, step] = (
                    acc_in[direction, piece, step - 1].astype(F32)
                    + dkv[owner, piece].astype(F32)
                ).astype(BF16)
                ring_copy(direction, piece, steps, step).start()
        add_cross(groups[step])

    def kv_copy(piece, p):
        return remote(
            final.at[piece, p // 2, pl.ds((p % 2) * TOK, TOK), :],
            cols((gk, gv)[piece], me, HD),
            kv_s.at[piece, p], kv_r.at[piece, me], device(y, p // 2, z, p % 2),
        )

    def kv_recv(piece, s):
        return remote(
            final.at[piece, s // 2, pl.ds((s % 2) * TOK, TOK), :],
            cols((gk, gv)[piece], s, HD),
            kv_s.at[piece, s], kv_r.at[piece, s], device(y, s // 2, z, s % 2),
        )

    kv_local = []
    for piece in (0, 1):
        last = [(d, steps) for d, pc, steps in CHAINS if pc == piece]
        for direction, steps in last:
            ring_copy(direction, piece, steps, steps - 1).wait_recv()
        (d0, s0), (d1, s1) = last
        final[piece] = (
            acc_in[d0, piece, s0 - 1].astype(F32)
            + acc_in[d1, piece, s1 - 1].astype(F32)
            + dkv[z, piece].astype(F32)
        ).astype(BF16)
        for p in slots[:-1]:
            kv_copy(piece, p).start()
        local = pltpu.make_async_copy(
            final.at[piece, x, pl.ds(core * TOK, TOK), :], cols((gk, gv)[piece], me, HD), kv_l.at[piece]
        )
        local.start()
        kv_local.append(local)

    @pl.when(y == 1)
    def _():
        for s in slots:
            cross_copy(s).wait_send()

    for direction, piece, steps in CHAINS:
        for step in range(steps):
            ring_copy(direction, piece, steps, step).wait_send()
    for p in slots[:-1]:
        q_copy(total, p).wait_send()
        q_recv(p).wait_recv()
        for piece in (0, 1):
            kv_copy(piece, p).wait_send()
            kv_recv(piece, p).wait_recv()
    q_local.wait()
    for c in kv_local:
        c.wait()


def give(dq, dkv):
    vmem = pl.BlockSpec(memory_space=pltpu.VMEM)
    dma = pltpu.SemaphoreType.DMA
    return pl.pallas_call(
        give_kernel,
        out_shape=(
            jax.ShapeDtypeStruct((TOK, QH * HD), BF16),
            jax.ShapeDtypeStruct((TOK, KVH * HD), BF16),
            jax.ShapeDtypeStruct((TOK, KVH * HD), BF16),
        ),
        in_specs=[vmem] * 2,
        out_specs=(vmem,) * 3,
        scratch_shapes=[
            pltpu.VMEM((PEERS, TOK, GW), BF16),
            pltpu.VMEM((PEERS, TOK, GW), BF16),
            pltpu.VMEM((2, 2, 4, NX, PIECE, HD), BF16),
            pltpu.VMEM((2, 2, 4, NX, PIECE, HD), BF16),
            pltpu.VMEM((2, NX, PIECE, HD), BF16),
            dma((PEERS,)), dma((PEERS,)),
            dma((2, 2, 4)), dma((2, 2, 4)),
            dma((PEERS,)), dma((PEERS,)), dma,
            dma((2, PEERS)), dma((2, PEERS)), dma((2,)),
        ],
        compiler_params=pltpu.CompilerParams(collective_id=1, has_side_effects=True, vmem_limit_bytes=16 << 20),
        name="give",
    )(dq, dkv)


def local(query_act, key_act, value_act, attn_out, grad_out, log_sum, kv_lists):
    args = (query_act, key_act, value_act, attn_out, grad_out, log_sum, kv_lists)
    qg, dog, stg, lsg, kvg = gather(
        *(pltpu.with_memory_space_constraint(a, pltpu.HBM) for a in args)
    )
    dq, dkv = attend(lsg, qg, dog, stg, kvg)
    return give(dq, dkv)


def solution(mesh):
    row = P(("blk", "head"), None)
    return jax.shard_map(
        local,
        mesh=mesh,
        in_specs=(row,) * 6 + (P("blk", None),),
        out_specs=(row,) * 3,
        check_vma=False,
    )
```

profile of v0, /device:TPU:9, one launch (start us, length us, event | category | flops | bytes accessed | tf_op | source)
XLA Modules:
  0.0 82.6 jit_solution(14692572912881839545)
XLA Ops:
  0.6 31.8 %gather.1 = (bf16[2,8,32,640]{3,2,1,0:T(8,128)(2,1)S(1)}, bf16[2,8,32,640]{3,2,1,0:T(8,128)(2,1)S(1)}, f32[2,8,32,128]{3,2,1,0:T(8,128)S(1)}, s32[2,4,8,128]{3,2...) custom-call(bf16[32,5120]{1,0:T(8,128)(2,1)} %q.1, bf16[32,1024]{1,0:T(8,128)(2,1)} %k.1, bf16[32,1024]{1,0:T(8,128)(2,1)} %v.1, ...), custom_call_target="tpu_custom_call" | custom-call | tf_op jit(solution)/shard_map/gather/pallas_call | solution.py:326
  32.4 25.7 %attend.1 = (bf16[2,8,32,640]{3,2,1,0:T(8,128)(2,1)S(1)}, bf16[8,2,4,64,128]{4,3,2,1,0:T(8,128)(2,1)S(1)}) custom-call(s32[2,4,8,128]{3,2,1,0:T(8,128)S(1)} %get-tuple-element.10.lists, bf16[2,8,32,640]{3,2,1,0:T(8,128)(2,1)S(1)} %get-tuple-element.11.qg, bf16[2,8,32,640]{3,2,1,0:T(8,128)(2,1)S(1)} %get-tuple-element.12.dog, ...), custom_call_target="tpu_custom_call" | custom-call | tf_op jit(solution)/shard_map/attend/pallas_call | solution.py:473
  58.1 22.5 %give.1 = (bf16[32,5120]{1,0:T(8,128)(2,1)S(1)}, bf16[32,1024]{1,0:T(8,128)(2,1)S(1)}, bf16[32,1024]{1,0:T(8,128)(2,1)S(1)}) custom-call(bf16[2,8,32,640]{3,2,1,0:T(8,128)(2,1)S(1)} %get-tuple-element.15.dq, bf16[8,2,4,64,128]{4,3,2,1,0:T(8,128)(2,1)S(1)} %get-tuple-element.16.dkv), custom_call_target="tpu_custom_call" | custom-call | tf_op jit(solution)/shard_map/give/pallas_call | solution.py:636
  80.6 0.7 copy.13
  81.3 0.6 copy.14
  82.0 0.6 copy.15
where the time goes:
time: 81.9 us; the launch traced here: 82.6 us
  Pallas kernels  80 us (98%)
  local copies, waits for them, and re-layouts  1.98 us (2%)
    pallas_call x1, Pallas kernels, gather(): pl.pallas_call(gather_kernel, out_shape=(jax.ShapeDtypeStruct((2, PEERS,...  31.8 us
    pallas_call x1, Pallas kernels, attend(): pl.pallas_call(attend_kernel, out_shape=(jax.ShapeDtypeStruct((2, PEERS,...  25.7 us
    pallas_call x1, Pallas kernels, give(): pl.pallas_call(give_kernel, out_shape=(jax.ShapeDtypeStruct((TOK, QH * HD...  22.5 us
    unnamed x3, local copies, waits for them, and re-layouts  1.98 us

commit v1 on v0

--- a/solution.py
+++ b/solution.py
@@ -72,13 +72,111 @@
 CHAINS = ((0, 0, 4), (0, 1, 3), (1, 1, 4), (1, 0, 3))
 
 
+BIG = 1e30
+ALLROWS = NX * ROWS
+
+
+def rows_of(x):
+    return slice(x * ROWS, (x + 1) * ROWS)
+
+
+def seen_bias(lists, part, x, half, base):
+    entries = lists[part, x, pl.ds(half, 1), :]
+    block = base + lax.broadcasted_iota(jnp.int32, (16, 128), 0)
+    hit = jnp.max(jnp.where(entries == block, 1.0, 0.0), axis=1, keepdims=True)
+    return jnp.broadcast_to(hit, (16, 128))
+
+
+def load_rows(x, part, qg, dog, stg, eye, qs, dos, qt, dot, lseb, delb):
+    for c in range(2):
+        st = stg[part, x * 2 + c]
+        for r in range(GS):
+            start = x * ROWS + r * PIECE + c * TOK
+            at = slice(start, start + TOK)
+            col = slice(r * HD, (r + 1) * HD)
+            qs[at, :] = qg[part, x * 2 + c, :, col]
+            dos[at, :] = dog[part, x * 2 + c, :, col]
+            lseb[at, :] = jnp.broadcast_to(st[:, r : r + 1], (TOK, 128))
+            delb[at, :] = jnp.broadcast_to(st[:, 8 + r : 9 + r], (TOK, 128))
+
+
+def turn_rows(lo, hi, eye, qs, dos, qt, dot):
+    at = slice(lo * ROWS, hi * ROWS)
+    qt[:, at] = lax.dot_general(eye, qs[at, :], NT, preferred_element_type=F32).astype(BF16)
+    dot[:, at] = lax.dot_general(eye, dos[at, :], NT, preferred_element_type=F32).astype(BF16)
+
+
+def identity():
+    r_id = lax.broadcasted_iota(jnp.int32, (128, 128), 0)
+    c_id = lax.broadcasted_iota(jnp.int32, (128, 128), 1)
+    return jnp.where(r_id == c_id, 1.0, 0.0).astype(BF16)
+
+
+def key_block(kvg, piece, b):
+    zz = (b % 4) * 2
+    return jnp.concatenate([kvg[zz, piece, b // 4], kvg[zz + 1, piece, b // 4]], axis=0)
+
+
+def tile(xs, a, b, kvg, bias, diag, qs, dos, qt, dot, lseb, delb, pbuf, dsbuf, dqa, dka, dva):
+    keys = jnp.concatenate([key_block(kvg, 0, a), key_block(kvg, 0, b)], axis=0)
+    values = jnp.concatenate([key_block(kvg, 1, a), key_block(kvg, 1, b)], axis=0)
+    for x in xs:
+        at = rows_of(x)
+        s = lax.dot_general(qs[at, :], keys, NT, preferred_element_type=F32)
+        dp = lax.dot_general(dos[at, :], values, NT, preferred_element_type=F32)
+        lse_a = lseb[at, :] + bias[x, pl.ds(a, 1), :]
+        lse_b = lseb[at, :] + bias[x, pl.ds(b, 1), :]
+        if diag is not None:
+            if x % 2 == 0 and x == xs[0]:
+                lse_a = lse_a + diag[...]
+            if x % 2 == 1 and x == xs[0] + 1:
+                lse_b = lse_b + diag[...]
+        p = jnp.exp2(s * (SCALE * LOG2E) - jnp.concatenate([lse_a, lse_b], axis=1))
+        delta = delb[at, :]
+        ds = (p * (dp - jnp.concatenate([delta, delta], axis=1))).astype(BF16)
+        pbuf[at, :] = p.astype(BF16)
+        dsbuf[at, :] = ds
+        dqa[at, :] += lax.dot_general(ds, keys, NN, preferred_element_type=F32)
+    at = slice(xs[0] * ROWS, (xs[-1] + 1) * ROWS)
+    dvt = lax.dot_general(dot[:, at], pbuf[at, :], NN, preferred_element_type=F32)
+    dkt = lax.dot_general(qt[:, at], dsbuf[at, :], NN, preferred_element_type=F32)
+    dva[a] += dvt[:, :BLOCK]
+    dka[a] += dkt[:, :BLOCK]
+    dva[b] += dvt[:, BLOCK:]
+    dka[b] += dkt[:, BLOCK:]
+
+
+def put_dq(dq, dqa):
+    for x in range(NX):
+        for c in range(2):
+            for r in range(GS):
+                start = x * ROWS + r * PIECE + c * TOK
+                dq[x * 2 + c, :, r * HD : (r + 1) * HD] = (
+                    dqa[start : start + TOK, :] * SCALE
+                ).astype(BF16)
+
+
+TILE_SCRATCH = [
+    pltpu.VMEM((ALLROWS, HD), BF16),
+    pltpu.VMEM((ALLROWS, HD), BF16),
+    pltpu.VMEM((HD, ALLROWS), BF16),
+    pltpu.VMEM((HD, ALLROWS), BF16),
+    pltpu.VMEM((ALLROWS, 128), F32),
+    pltpu.VMEM((ALLROWS, 128), F32),
+    pltpu.VMEM((ALLROWS, 2 * BLOCK), BF16),
+    pltpu.VMEM((ALLROWS, 2 * BLOCK), BF16),
+    pltpu.VMEM((ALLROWS, HD), F32),
+]
+
+
 NEAR = ((0, 1), (1, 0), (3, 0), (1, 1), (3, 1), (2, 0), (2, 1))
 
 
 def gather_kernel(
     q, k, v, o, do, lse, lists,
-    qg, dog, stg, lsg, kvg,
-    o_buf, do_buf, lse_buf, rows_buf, stat_src, list_src, in_sem,
+    qg, dog, stg, kvg, dq, dka, dva, far_bias, far_any,
+    o_buf, do_buf, lse_buf, rows_buf, stat_src, list_src, lsg, bias, diag,
+    qs, dos, qt, dot, lseb, delb, pbuf, dsbuf, dqa, in_sem,
     kv_s, kv_r, kv_l, big_s, big_r, big_l, st_s, st_r, st_l, ls_s, ls_r, ls_l,
     ring_s, ring_r, cr_s, cr_r, crst_s, crst_r, crls_s, crls_r,
 ):
@@ -167,15 +265,8 @@
         c.start()
 
     loads[0].wait()
-    rows = rows_buf[...]
-    count = jnp.sum(jnp.where(rows >= 0, 1.0, 0.0), axis=1, keepdims=True).astype(jnp.int32)
-    early = jnp.sum(
-        jnp.where((rows >= 0) & (rows < 32), 1.0, 0.0), axis=1, keepdims=True
-    ).astype(jnp.int32)
-    list_src[...] = jnp.zeros((8, 128), jnp.int32)
-    list_src[0:2, 0:LISTW] = rows
-    lane = lax.broadcasted_iota(jnp.int32, (2, 128), 1)
-    list_src[4:6, :] = jnp.where(lane == 0, count, early)
+    list_src[...] = jnp.full((8, 128), -1, jnp.int32)
+    list_src[0:2, 0:LISTW] = rows_buf[...]
 
     for c in loads[1:]:
         c.wait()
@@ -192,6 +283,16 @@
             block = jnp.where(lane == 8 + r, delta, block)
         stat_src[g] = block
 
+    for ref in (dka, dva, dqa):
+        ref[...] = jnp.zeros_like(ref)
+    eye = identity()
+    half = (z % 4) // 2
+    base = y * 16
+    row_tok = (z % 2) * PIECE + lax.broadcasted_iota(jnp.int32, (ROWS, 128), 0) % PIECE
+    key_tok = lax.broadcasted_iota(jnp.int32, (ROWS, 128), 1)
+    diag[0] = jnp.where(key_tok <= row_tok, 0.0, BIG)
+    diag[1] = jnp.zeros((ROWS, 128), F32)
+
     wait_peers(bar, y)
     for piece in (0, 1):
         for n in NEAR[1:] + NEAR[:1]:
@@ -287,9 +388,34 @@
         crst.start()
         crls.start()
 
-    for step in (2, 3):
-        for piece in (0, 1):
-            ring_step(step, piece)
+    state = (qs, dos, qt, dot, lseb, delb)
+    for piece in (0, 1):
+        for i in (0, 1):
+            load_rows(piece * 2 + i, 0, qg, dog, stg, eye, *state)
+        turn_rows(piece * 2, piece * 2 + 2, eye, *state[:4])
+        ring_step(2, piece)
+    for xx in range(NX):
+        bias[xx] = jnp.where(seen_bias(lsg, 0, xx, half, base) > 0.0, 0.0, BIG)
+
+    own = z // 2
+    side = (z % 2) * 2 - 1
+
+    def column(i, carry):
+        @pl.when(i == 3)
+        def _():
+            ring_step(3, 0)
+            ring_step(3, 1)
+
+        move = jnp.where(i == 1, side, jnp.where(i == 2, -side, jnp.where(i == 3, 2, 0)))
+        zz = (own + move + 4) % 4
+        cut = diag.at[jnp.where(i == 0, 0, 1)]
+        rest = (pbuf, dsbuf, dqa, dka, dva)
+        tile((0, 1, 2, 3), zz, zz + 4, kvg, bias, cut, *state, *rest)
+        tile((2, 3), zz + 8, zz + 12, kvg, bias, cut, *state, *rest)
+        return carry
+
+    lax.fori_loop(0, 4, column, 0)
+    put_dq(dq, dqa)
 
     for n in NEAR:
         for i in (0, 1):
@@ -317,6 +443,11 @@
                 cross_copy(s, which).wait_recv()
         crst.wait_recv()
         crls.wait_recv()
+        hits = [seen_bias(lsg, 1, xx, half, base) for xx in range(NX)]
+        for xx in range(NX):
+            far_bias[xx] = jnp.where(hits[xx] > 0.0, 0.0, BIG)
+        some = jnp.maximum(jnp.maximum(hits[0], hits[1]), jnp.maximum(hits[2], hits[3]))
+        far_any[...] = some.astype(jnp.int32)
 
 
 def gather(q, k, v, o, do, lse, lists):
@@ -329,11 +460,15 @@
             jax.ShapeDtypeStruct((2, PEERS, TOK, GW), BF16),
             jax.ShapeDtypeStruct((2, PEERS, TOK, GW), BF16),
             jax.ShapeDtypeStruct((2, PEERS, TOK, 128), F32),
-            jax.ShapeDtypeStruct((2, NX, 8, 128), jnp.int32),
             jax.ShapeDtypeStruct((NZ, 2, NX, PIECE, HD), BF16),
+            jax.ShapeDtypeStruct((PEERS, TOK, GW), BF16),
+            jax.ShapeDtypeStruct((16, HD, BLOCK), F32),
+            jax.ShapeDtypeStruct((16, HD, BLOCK), F32),
+            jax.ShapeDtypeStruct((NX, 16, 128), F32),
+            jax.ShapeDtypeStruct((16, 128), jnp.int32),
         ),
         in_specs=[hbm] * 7,
-        out_specs=(vmem,) * 5,
+        out_specs=(vmem,) * 9,
         scratch_shapes=[
             pltpu.VMEM((TOK, QH * HD), BF16),
             pltpu.VMEM((TOK, QH * HD), BF16),
@@ -341,6 +476,10 @@
             pltpu.VMEM((2, LISTW), jnp.int32),
             pltpu.VMEM((KVH, TOK, 128), F32),
             pltpu.VMEM((8, 128), jnp.int32),
+            pltpu.VMEM((2, NX, 8, 128), jnp.int32),
+            pltpu.VMEM((NX, 16, 128), F32),
+            pltpu.VMEM((2, ROWS, 128), F32),
+            *TILE_SCRATCH,
             dma((4,)),
             dma((2, PEERS)), dma((2, PEERS)), dma((2,)),
             dma((2, PEERS)), dma((2, PEERS)), dma((2,)),
@@ -351,151 +490,90 @@
             dma, dma, dma, dma,
         ],
         compiler_params=pltpu.CompilerParams(
-            collective_id=0, has_side_effects=True, vmem_limit_bytes=16 << 20
+            collective_id=0, has_side_effects=True, vmem_limit_bytes=24 << 20
         ),
         name="gather",
     )(q, k, v, o, do, lse, lists)
 
 
-def attend_kernel(
-    lists, qg, dog, stg, kvg, dq, dkv,
-    qs, dos, qt, dot, lseb, delb, dqa, dka, dva,
+def far_kernel(
+    far_any, qg, dog, stg, kvg, far_bias, dka_in, dva_in, dq, dkv,
+    order, qs, dos, qt, dot, lseb, delb, pbuf, dsbuf, dqa, dka, dva,
 ):
     y, x, z, core = coords()
-    half = (z % 4) // 2
-    base = y * 16
-    for ref in (dka, dva):
-        ref[...] = jnp.zeros_like(ref)
-    r_id = lax.broadcasted_iota(jnp.int32, (128, 128), 0)
-    c_id = lax.broadcasted_iota(jnp.int32, (128, 128), 1)
-    eye = jnp.where(r_id == c_id, 1.0, 0.0).astype(BF16)
-    row_tok = (z % 2) * PIECE + lax.broadcasted_iota(jnp.int32, (ROWS, 128), 0) % PIECE
-    key_tok = lax.broadcasted_iota(jnp.int32, (ROWS, 128), 1)
-
-    def chunk(i, carry):
-        part = i // NX
-        xx = i % NX
-        total = lists[part, xx, 4 + half, 0]
-        early = lists[part, xx, 4 + half, 1]
-        own = part == 0
-        lo = jnp.where(own & (y == 2), early, 0)
-        hi = jnp.where(own, total, jnp.where(y == 1, early, 0))
-        n = hi - lo
-        diag = jnp.where(own, xx * 4 + z // 2, -1)
-
-        @pl.when(n > 0)
-        def _():
-            for c in range(2):
-                st = stg[part, xx * 2 + c]
-                for r in range(GS):
-                    at = slice(r * PIECE + c * TOK, r * PIECE + (c + 1) * TOK)
-                    col = slice(r * HD, (r + 1) * HD)
-                    qs[at, :] = qg[part, xx * 2 + c, :, col]
-                    dos[at, :] = dog[part, xx * 2 + c, :, col]
-                    lseb[at, :] = jnp.broadcast_to(st[:, r : r + 1], (TOK, 128))
-                    delb[at, :] = jnp.broadcast_to(st[:, 8 + r : 9 + r], (TOK, 128))
-            qt[...] = lax.dot_general(eye, qs[...], NT, preferred_element_type=F32).astype(BF16)
-            dot[...] = lax.dot_general(eye, dos[...], NT, preferred_element_type=F32).astype(BF16)
-            dqa[...] = jnp.zeros_like(dqa)
-
-            def block(piece, b):
-                zz = (b % 4) * 2
-                return jnp.concatenate(
-                    [kvg[zz, piece, b // 4], kvg[zz + 1, piece, b // 4]], axis=0
-                )
-
-            def pair(j, masked):
-                a = lists[part, xx, half, j] - base
-                if masked:
-                    has = j + 1 < hi
-                    b = jnp.where(has, lists[part, xx, half, jnp.where(has, j + 1, j)] - base, a)
-                else:
-                    b = lists[part, xx, half, j + 1] - base
-                keys = jnp.concatenate([block(0, a), block(0, b)], axis=0)
-                values = jnp.concatenate([block(1, a), block(1, b)], axis=0)
-                s = lax.dot_general(qs[...], keys, NT, preferred_element_type=F32)
-                lse2 = jnp.concatenate([lseb[...], lseb[...]], axis=1)
-                del2 = jnp.concatenate([delb[...], delb[...]], axis=1)
-                p = jnp.exp2(s * (SCALE * LOG2E) - lse2)
-                if masked:
-                    ta = row_tok + jnp.where(a == diag, 0, BLOCK)
-                    tb = row_tok + jnp.where(has, jnp.where(b == diag, 0, BLOCK), -2 * BLOCK)
-                    seen = jnp.concatenate([key_tok <= ta, key_tok <= tb], axis=1)
-                    p = jnp.where(seen, p, 0.0)
-                dp = lax.dot_general(dos[...], values, NT, preferred_element_type=F32)
-                ds = (p * (dp - del2)).astype(BF16)
-                pb = p.astype(BF16)
-                dvt = lax.dot_general(dot[...], pb, NN, preferred_element_type=F32)
-                dkt = lax.dot_general(qt[...], ds, NN, preferred_element_type=F32)
-                dqa[...] += lax.dot_general(ds, keys, NN, preferred_element_type=F32)
-                dva[a] += dvt[:, :BLOCK]
-                dka[a] += dkt[:, :BLOCK]
-                dva[b] += dvt[:, BLOCK:]
-                dka[b] += dkt[:, BLOCK:]
-
-            full = (n - 1) // 2
-
-            def step(t, carry):
-                pair(lo + 2 * t, False)
-                return carry
-
-            lax.fori_loop(0, full, step, 0)
-            pair(lo + 2 * full, True)
-            for c in range(2):
-                for r in range(GS):
-                    at = slice(r * PIECE + c * TOK, r * PIECE + (c + 1) * TOK)
-                    col = slice(r * HD, (r + 1) * HD)
-                    dq[part, xx * 2 + c, :, col] = (dqa[at, :] * SCALE).astype(BF16)
-
-        @pl.when((n <= 0) & (y == 1))
-        def _():
-            for c in range(2):
-                dq[part, xx * 2 + c] = jnp.zeros((TOK, GW), BF16)
-
-        return carry
-
-    lax.fori_loop(0, jnp.where(y == 1, 2 * NX, NX), chunk, 0)
-
-    def finish(b, carry):
-        zz = (b % 4) * 2
-        for piece, ref, scale in ((0, dka, SCALE), (1, dva, 1.0)):
-            low = (ref[b] * scale).astype(BF16)
-            out = lax.dot_general(eye, low, NT, preferred_element_type=F32).astype(BF16)
-            dkv[zz, piece, b // 4] = out[:PIECE]
-            dkv[zz + 1, piece, b // 4] = out[PIECE:]
-        return carry
-
-    lax.fori_loop(0, 16, finish, 0)
-
-
-def attend(lists, qg, dog, stg, kvg):
+    eye = identity()
+
+    def finish(kref, vref):
+        def one(b, carry):
+            zz = (b % 4) * 2
+            for piece, ref, scale in ((0, kref, SCALE), (1, vref, 1.0)):
+                low = (ref[b] * scale).astype(BF16)
+                out = lax.dot_general(eye, low, NT, preferred_element_type=F32).astype(BF16)
+                dkv[zz, piece, b // 4] = out[:PIECE]
+                dkv[zz + 1, piece, b // 4] = out[PIECE:]
+            return carry
+
+        lax.fori_loop(0, 16, one, 0)
+
+    @pl.when(y == 1)
+    def _():
+        def note(b, n):
+            order[n] = b
+            return n + (far_any[b, 0] > 0).astype(jnp.int32)
+
+        n = lax.fori_loop(0, 16, note, 0)
+
+        def unseen(b, first):
+            return jnp.where(far_any[b, 0] > 0, first, b)
+
+        order[n] = lax.fori_loop(0, 16, unseen, 0)
+        state = (qs, dos, qt, dot, lseb, delb)
+        for xx in range(NX):
+            load_rows(xx, 1, qg, dog, stg, eye, *state)
+        turn_rows(0, NX, eye, *state[:4])
+        for ref, src in ((dka, dka_in), (dva, dva_in)):
+            ref[...] = src[...]
+        dqa[...] = jnp.zeros_like(dqa)
+
+        def pair(i, carry):
+            tile(
+                (0, 1, 2, 3), order[2 * i], order[2 * i + 1], kvg, far_bias, None,
+                *state, pbuf, dsbuf, dqa, dka, dva,
+            )
+            return carry
+
+        lax.fori_loop(0, (n + 1) // 2, pair, 0)
+        put_dq(dq, dqa)
+        finish(dka, dva)
+
+    @pl.when(y != 1)
+    def _():
+        finish(dka_in, dva_in)
+
+
+def far(far_any, *args):
     vmem = pl.BlockSpec(memory_space=pltpu.VMEM)
     return pl.pallas_call(
-        attend_kernel,
+        far_kernel,
         out_shape=(
-            jax.ShapeDtypeStruct((2, PEERS, TOK, GW), BF16),
+            jax.ShapeDtypeStruct((PEERS, TOK, GW), BF16),
             jax.ShapeDtypeStruct((NZ, 2, NX, PIECE, HD), BF16),
         ),
-        in_specs=[pl.BlockSpec(memory_space=pltpu.SMEM)] + [vmem] * 4,
+        in_specs=[pl.BlockSpec(memory_space=pltpu.SMEM)] + [vmem] * 7,
         out_specs=(vmem, vmem),
         scratch_shapes=[
-            pltpu.VMEM((ROWS, HD), BF16),
-            pltpu.VMEM((ROWS, HD), BF16),
-            pltpu.VMEM((HD, ROWS), BF16),
-            pltpu.VMEM((HD, ROWS), BF16),
-            pltpu.VMEM((ROWS, 128), F32),
-            pltpu.VMEM((ROWS, 128), F32),
-            pltpu.VMEM((ROWS, HD), F32),
+            pltpu.SMEM((32,), jnp.int32),
+            *TILE_SCRATCH,
             pltpu.VMEM((16, HD, BLOCK), F32),
             pltpu.VMEM((16, HD, BLOCK), F32),
         ],
-        compiler_params=pltpu.CompilerParams(vmem_limit_bytes=16 << 20),
-        name="attend",
-    )(lists, qg, dog, stg, kvg)
+        compiler_params=pltpu.CompilerParams(vmem_limit_bytes=24 << 20),
+        name="far",
+    )(far_any, *args)
 
 
 def give_kernel(
-    dq, dkv, gq, gk, gv,
+    dq, far_dq, dkv, gq, gk, gv,
     land, total, acc_in, acc_out, final,
     cr_s, cr_r, ring_s, ring_r, q_s, q_r, q_l, kv_s, kv_r, kv_l,
 ):
@@ -509,7 +587,7 @@
         return ref.at[:, pl.ds(pl.multiple_of(g * width, 128), width)]
 
     def cross_copy(s):
-        return remote(dq.at[1, s], land.at[s], cr_s.at[s], cr_r.at[s], device(3 - y, x, z, core))
+        return remote(far_dq.at[s], land.at[s], cr_s.at[s], cr_r.at[s], device(3 - y, x, z, core))
 
     slots = [(me + d) % PEERS for d in (2, 3, 4, 5, 6, 7, 1, 0)]
 
@@ -545,12 +623,12 @@
         )
 
     q_local = pltpu.make_async_copy(total.at[me], cols(gq, me, GW), q_l)
-    q_local_direct = pltpu.make_async_copy(dq.at[0, me], cols(gq, me, GW), q_l)
+    q_local_direct = pltpu.make_async_copy(dq.at[me], cols(gq, me, GW), q_l)
 
     @pl.when(y != 2)
     def _():
         for p in slots[:-1]:
-            q_copy(dq.at[0], p).start()
+            q_copy(dq, p).start()
         q_local_direct.start()
 
     def add_cross(some):
@@ -558,7 +636,7 @@
         def _():
             for s in some:
                 cross_copy(s).wait_recv()
-                total[s] = (dq[0, s].astype(F32) + land[s].astype(F32)).astype(BF16)
+                total[s] = (dq[s].astype(F32) + land[s].astype(F32)).astype(BF16)
                 if s is slots[-1]:
                     q_local.start()
                 else:
@@ -630,7 +708,7 @@
         c.wait()
 
 
-def give(dq, dkv):
+def give(dq, far_dq, dkv):
     vmem = pl.BlockSpec(memory_space=pltpu.VMEM)
     dma = pltpu.SemaphoreType.DMA
     return pl.pallas_call(
@@ -640,7 +718,7 @@
             jax.ShapeDtypeStruct((TOK, KVH * HD), BF16),
             jax.ShapeDtypeStruct((TOK, KVH * HD), BF16),
         ),
-        in_specs=[vmem] * 2,
+        in_specs=[vmem] * 3,
         out_specs=(vmem,) * 3,
         scratch_shapes=[
             pltpu.VMEM((PEERS, TOK, GW), BF16),
@@ -655,16 +733,16 @@
         ],
         compiler_params=pltpu.CompilerParams(collective_id=1, has_side_effects=True, vmem_limit_bytes=16 << 20),
         name="give",
-    )(dq, dkv)
+    )(dq, far_dq, dkv)
 
 
 def local(query_act, key_act, value_act, attn_out, grad_out, log_sum, kv_lists):
     args = (query_act, key_act, value_act, attn_out, grad_out, log_sum, kv_lists)
-    qg, dog, stg, lsg, kvg = gather(
+    qg, dog, stg, kvg, dq, dka, dva, far_bias, far_any = gather(
         *(pltpu.with_memory_space_constraint(a, pltpu.HBM) for a in args)
     )
-    dq, dkv = attend(lsg, qg, dog, stg, kvg)
-    return give(dq, dkv)
+    far_dq, dkv = far(far_any, qg, dog, stg, kvg, far_bias, dka, dva)
+    return give(dq, far_dq, dkv)
 
 
 def solution(mesh):

time: 81.9 us -> 72.3 us (0.88)
  Pallas kernels: 80 us -> 70.3 us
    pallas_call x1, Pallas kernels: 25.7 us -> 12 us  [far(): pl.pallas_call(far_kernel, out_shape=(jax.ShapeDtypeStruct((PEERS, TOK, G...]
    pallas_call x1, Pallas kernels: 31.8 us -> 34 us  [gather(): pl.pallas_call(gather_kernel, out_shape=(jax.ShapeDtypeStruct((2, PEERS,...]
    pallas_call x1, Pallas kernels: 22.5 us -> 24.3 us  [give(): pl.pallas_call(give_kernel, out_shape=(jax.ShapeDtypeStruct((TOK, QH * HD...]
where the time goes in v1:
time: 72.3 us; the launch traced here: 72.9 us
  Pallas kernels  70.3 us (97%)
  local copies, waits for them, and re-layouts  1.98 us (3%)
    pallas_call x1, Pallas kernels, gather(): pl.pallas_call(gather_kernel, out_shape=(jax.ShapeDtypeStruct((2, PEERS,...  34 us
    pallas_call x1, Pallas kernels, give(): pl.pallas_call(give_kernel, out_shape=(jax.ShapeDtypeStruct((TOK, QH * HD...  24.3 us
    pallas_call x1, Pallas kernels, far(): pl.pallas_call(far_kernel, out_shape=(jax.ShapeDtypeStruct((PEERS, TOK, G...  12 us
    unnamed x3, local copies, waits for them, and re-layouts  1.98 us

profile of v1, /device:TPU:9, one launch (start us, length us, event | category | flops | bytes accessed | tf_op | source)
XLA Modules:
  0.0 72.9 jit_solution(10625953290826078213)
XLA Ops:
  0.6 34.0 %gather.1 = (bf16[2,8,32,640]{3,2,1,0:T(8,128)(2,1)S(1)}, bf16[2,8,32,640]{3,2,1,0:T(8,128)(2,1)S(1)}, f32[2,8,32,128]{3,2,1,0:T(8,128)S(1)}, bf16[8,2,4,64,128]...) custom-call(bf16[32,5120]{1,0:T(8,128)(2,1)} %q.1, ...), custom_call_target="tpu_custom_call" | custom-call | tf_op jit(solution)/shard_map/gather/pallas_call | solution.py:457
  34.6 12.0 %far.1 = (bf16[8,32,640]{2,1,0:T(8,128)(2,1)S(1)}, bf16[8,2,4,64,128]{4,3,2,1,0:T(8,128)(2,1)S(1)}) custom-call(s32[16,128]{1,0:T(8,128)S(1)} %get-tuple-element.15.far_any, bf16[2,8,32,640]{3,2,1,0:T(8,128)(2,1)S(1)} %get-tuple-element.16.qg, bf16[2,8,32,640]{3,2,1,0:T(8,128)(2,1)S(1)} %get-tuple-element.17.dog, ...), custom_call_target="tpu_custom_call" | custom-call | tf_op jit(solution)/shard_map/far/pallas_call | solution.py:556
  46.6 24.3 %give.1 = (bf16[32,5120]{1,0:T(8,128)(2,1)S(1)}, bf16[32,1024]{1,0:T(8,128)(2,1)S(1)}, bf16[32,1024]{1,0:T(8,128)(2,1)S(1)}) custom-call(bf16[8,32,640]{2,1,0:T(8,128)(2,1)S(1)} %get-tuple-element.14.dq, bf16[8,32,640]{2,1,0:T(8,128)(2,1)S(1)} %get-tuple-element.23.far_dq, bf16[8,2,4,64,128]{4,3,2,1,0:T(8,128)(2,1)S(1)} %get-tuple-element.24.dkv), custom_call_target="tpu_custom_call" | custom-call | tf_op jit(solution)/shard_map/give/pallas_call | solution.py:714
  71.0 0.7 copy.13
  71.7 0.6 copy.14
  72.3 0.6 copy.15

commit v2 on v1

--- a/solution.py
+++ b/solution.py
@@ -172,13 +172,15 @@
 NEAR = ((0, 1), (1, 0), (3, 0), (1, 1), (3, 1), (2, 0), (2, 1))
 
 
-def gather_kernel(
+def whole_kernel(
     q, k, v, o, do, lse, lists,
-    qg, dog, stg, kvg, dq, dka, dva, far_bias, far_any,
+    gq, gk, gv,
+    qg, dog, stg, kvg, dq, far_dq, dka, dva, dkv, land, total, acc_in, acc_out, final,
     o_buf, do_buf, lse_buf, rows_buf, stat_src, list_src, lsg, bias, diag,
     qs, dos, qt, dot, lseb, delb, pbuf, dsbuf, dqa, in_sem,
     kv_s, kv_r, kv_l, big_s, big_r, big_l, st_s, st_r, st_l, ls_s, ls_r, ls_l,
     ring_s, ring_r, cr_s, cr_r, crst_s, crst_r, crls_s, crls_r,
+    dq_s, dq_r, red_s, red_r, out_s, out_r, out_l, kvo_s, kvo_r, kvo_l,
 ):
     y, x, z, core = coords()
     me = x * 2 + core
@@ -417,6 +419,162 @@
     lax.fori_loop(0, 4, column, 0)
     put_dq(dq, dqa)
 
+    def cross_dq(s):
+        return remote(far_dq.at[s], land.at[s], dq_s.at[s], dq_r.at[s], device(3 - y, x, z, core))
+
+    def dq_copy(src, p):
+        return remote(src.at[p], cols(gq, me, GW), out_s.at[p], out_r.at[me], at(p))
+
+    def dq_recv(s):
+        return remote(total.at[s], cols(gq, s, GW), out_s.at[s], out_r.at[s], at(s))
+
+    dq_local = pltpu.make_async_copy(total.at[me], cols(gq, me, GW), out_l)
+
+    @pl.when(y != 2)
+    def _():
+        for n in NEAR:
+            dq_copy(dq, to(n)).start()
+        pltpu.make_async_copy(dq.at[me], cols(gq, me, GW), out_l).start()
+
+    @pl.when(y == 1)
+    def _():
+        for s in range(PEERS):
+            for which in (0, 1):
+                cross_copy(s, which).wait_recv()
+        crst.wait_recv()
+        crls.wait_recv()
+        for xx in range(NX):
+            load_rows(xx, 1, qg, dog, stg, eye, *state)
+            bias[xx] = jnp.where(seen_bias(lsg, 1, xx, half, base) > 0.0, 0.0, BIG)
+        turn_rows(0, NX, eye, *state[:4])
+        dqa[...] = jnp.zeros_like(dqa)
+
+    def red_copy(direction, piece, steps, step):
+        sign = (1, NZ - 1)[direction]
+        owner = (z + sign * (steps - step)) % NZ
+        if step == 0:
+            src = dkv.at[owner, piece]
+        else:
+            src = acc_out.at[direction, piece, step]
+        return remote(
+            src, acc_in.at[direction, piece, step],
+            red_s.at[direction, piece, step], red_r.at[direction, piece, step],
+            device(y, x, (z + sign) % NZ, core),
+        )
+
+    def red_step(direction, piece, steps, step):
+        sign = (1, NZ - 1)[direction]
+        owner = (z + sign * (steps - step)) % NZ
+        red_copy(direction, piece, steps, step - 1).wait_recv()
+        acc_out[direction, piece, step] = (
+            acc_in[direction, piece, step - 1].astype(F32) + dkv[owner, piece].astype(F32)
+        ).astype(BF16)
+        red_copy(direction, piece, steps, step).start()
+
+    def finish(zz):
+        @pl.when(y == 1)
+        def _():
+            rest = (pbuf, dsbuf, dqa, dka, dva)
+            tile((0, 1, 2, 3), zz, zz + 4, kvg, bias, None, *state, *rest)
+            tile((0, 1, 2, 3), zz + 8, zz + 12, kvg, bias, None, *state, *rest)
+
+        for xx in range(NX):
+            for piece, ref, scale in ((0, dka, SCALE), (1, dva, 1.0)):
+                low = (ref[zz + 4 * xx] * scale).astype(BF16)
+                turned = lax.dot_general(eye, low, NT, preferred_element_type=F32).astype(BF16)
+                dkv[2 * zz, piece, xx] = turned[:PIECE]
+                dkv[2 * zz + 1, piece, xx] = turned[PIECE:]
+
+    long = ((0, 0, 4), (1, 1, 4))
+    short = ((0, 1, 3), (1, 0, 3))
+
+    def reduce_column(i, carry):
+        move = jnp.where(i == 0, 2, jnp.where(i == 1, -side, jnp.where(i == 2, side, 0)))
+        finish((own + move + 4) % 4)
+
+        @pl.when(i == 0)
+        def _():
+            for c in long:
+                red_copy(*c, 0).start()
+
+        @pl.when(i == 1)
+        def _():
+            for c in short:
+                red_copy(*c, 0).start()
+            for c in long:
+                red_step(*c, 1)
+
+        @pl.when(i == 2)
+        def _():
+            for c in short:
+                red_step(*c, 1)
+            for c in long:
+                red_step(*c, 2)
+
+        return carry
+
+    lax.fori_loop(0, 4, reduce_column, 0)
+
+    @pl.when(y == 1)
+    def _():
+        put_dq(far_dq, dqa)
+        for s in range(PEERS):
+            cross_dq(s).start()
+
+    for c in short:
+        red_step(*c, 2)
+    for c in long:
+        red_step(*c, 3)
+
+    def grad_copy(piece, p):
+        return remote(
+            final.at[piece, p // 2, pl.ds((p % 2) * TOK, TOK), :],
+            cols((gk, gv)[piece], me, HD),
+            kvo_s.at[piece, p], kvo_r.at[piece, me], at(p),
+        )
+
+    def grad_recv(piece, s):
+        return remote(
+            final.at[piece, s // 2, pl.ds((s % 2) * TOK, TOK), :],
+            cols((gk, gv)[piece], s, HD),
+            kvo_s.at[piece, s], kvo_r.at[piece, s], at(s),
+        )
+
+    grad_local = []
+    for piece in (0, 1):
+        (d0, s0), (d1, s1) = [(d, steps) for d, pc, steps in CHAINS if pc == piece]
+        red_copy(d0, piece, s0, s0 - 1).wait_recv()
+        red_copy(d1, piece, s1, s1 - 1).wait_recv()
+        final[piece] = (
+            acc_in[d0, piece, s0 - 1].astype(F32)
+            + acc_in[d1, piece, s1 - 1].astype(F32)
+            + dkv[z, piece].astype(F32)
+        ).astype(BF16)
+        for n in NEAR:
+            grad_copy(piece, to(n)).start()
+        grad_local.append(
+            pltpu.make_async_copy(
+                final.at[piece, x, pl.ds(core * TOK, TOK), :],
+                cols((gk, gv)[piece], me, HD), kvo_l.at[piece],
+            )
+        )
+        grad_local[piece].start()
+
+    @pl.when(y == 2)
+    def _():
+        for s in range(PEERS):
+            cross_dq(s).wait_recv()
+            total[s] = (dq[s].astype(F32) + land[s].astype(F32)).astype(BF16)
+
+            @pl.when(s == me)
+            def _():
+                dq_local.start()
+
+            @pl.when(s != me)
+            def _():
+                dq_copy(total, s).start()
+
+
     for n in NEAR:
         for i in (0, 1):
             kv_copy(to(n), i).wait_send()
@@ -436,40 +594,54 @@
         crst.wait_send()
         crls.wait_send()
 
+
     @pl.when(y == 1)
     def _():
         for s in range(PEERS):
-            for which in (0, 1):
-                cross_copy(s, which).wait_recv()
-        crst.wait_recv()
-        crls.wait_recv()
-        hits = [seen_bias(lsg, 1, xx, half, base) for xx in range(NX)]
-        for xx in range(NX):
-            far_bias[xx] = jnp.where(hits[xx] > 0.0, 0.0, BIG)
-        some = jnp.maximum(jnp.maximum(hits[0], hits[1]), jnp.maximum(hits[2], hits[3]))
-        far_any[...] = some.astype(jnp.int32)
-
-
-def gather(q, k, v, o, do, lse, lists):
+            cross_dq(s).wait_send()
+
+    for direction, piece, steps in CHAINS:
+        for step in range(steps):
+            red_copy(direction, piece, steps, step).wait_send()
+    for n in NEAR:
+        for piece in (0, 1):
+            grad_copy(piece, to(n)).wait_send()
+            grad_recv(piece, of(n)).wait_recv()
+        dq_copy(total, to(n)).wait_send()
+        dq_recv(of(n)).wait_recv()
+    for c in grad_local:
+        c.wait()
+    dq_local.wait()
+
+
+def whole(*args):
     vmem = pl.BlockSpec(memory_space=pltpu.VMEM)
     hbm = pl.BlockSpec(memory_space=pltpu.HBM)
     dma = pltpu.SemaphoreType.DMA
     return pl.pallas_call(
-        gather_kernel,
+        whole_kernel,
         out_shape=(
-            jax.ShapeDtypeStruct((2, PEERS, TOK, GW), BF16),
-            jax.ShapeDtypeStruct((2, PEERS, TOK, GW), BF16),
-            jax.ShapeDtypeStruct((2, PEERS, TOK, 128), F32),
-            jax.ShapeDtypeStruct((NZ, 2, NX, PIECE, HD), BF16),
-            jax.ShapeDtypeStruct((PEERS, TOK, GW), BF16),
-            jax.ShapeDtypeStruct((16, HD, BLOCK), F32),
-            jax.ShapeDtypeStruct((16, HD, BLOCK), F32),
-            jax.ShapeDtypeStruct((NX, 16, 128), F32),
-            jax.ShapeDtypeStruct((16, 128), jnp.int32),
+            jax.ShapeDtypeStruct((TOK, QH * HD), BF16),
+            jax.ShapeDtypeStruct((TOK, KVH * HD), BF16),
+            jax.ShapeDtypeStruct((TOK, KVH * HD), BF16),
         ),
         in_specs=[hbm] * 7,
-        out_specs=(vmem,) * 9,
+        out_specs=(vmem,) * 3,
         scratch_shapes=[
+            pltpu.VMEM((2, PEERS, TOK, GW), BF16),
+            pltpu.VMEM((2, PEERS, TOK, GW), BF16),
+            pltpu.VMEM((2, PEERS, TOK, 128), F32),
+            pltpu.VMEM((NZ, 2, NX, PIECE, HD), BF16),
+            pltpu.VMEM((PEERS, TOK, GW), BF16),
+            pltpu.VMEM((PEERS, TOK, GW), BF16),
+            pltpu.VMEM((16, HD, BLOCK), F32),
+            pltpu.VMEM((16, HD, BLOCK), F32),
+            pltpu.VMEM((NZ, 2, NX, PIECE, HD), BF16),
+            pltpu.VMEM((PEERS, TOK, GW), BF16),
+            pltpu.VMEM((PEERS, TOK, GW), BF16),
+            pltpu.VMEM((2, 2, 4, NX, PIECE, HD), BF16),
+            pltpu.VMEM((2, 2, 4, NX, PIECE, HD), BF16),
+            pltpu.VMEM((2, NX, PIECE, HD), BF16),
             pltpu.VMEM((TOK, QH * HD), BF16),
             pltpu.VMEM((TOK, QH * HD), BF16),
             pltpu.VMEM((TOK, QH), F32),
@@ -488,261 +660,21 @@
             dma((2, 2, 4)), dma((2, 2, 4)),
             dma((2, PEERS)), dma((2, PEERS)),
             dma, dma, dma, dma,
-        ],
-        compiler_params=pltpu.CompilerParams(
-            collective_id=0, has_side_effects=True, vmem_limit_bytes=24 << 20
-        ),
-        name="gather",
-    )(q, k, v, o, do, lse, lists)
-
-
-def far_kernel(
-    far_any, qg, dog, stg, kvg, far_bias, dka_in, dva_in, dq, dkv,
-    order, qs, dos, qt, dot, lseb, delb, pbuf, dsbuf, dqa, dka, dva,
-):
-    y, x, z, core = coords()
-    eye = identity()
-
-    def finish(kref, vref):
-        def one(b, carry):
-            zz = (b % 4) * 2
-            for piece, ref, scale in ((0, kref, SCALE), (1, vref, 1.0)):
-                low = (ref[b] * scale).astype(BF16)
-                out = lax.dot_general(eye, low, NT, preferred_element_type=F32).astype(BF16)
-                dkv[zz, piece, b // 4] = out[:PIECE]
-                dkv[zz + 1, piece, b // 4] = out[PIECE:]
-            return carry
-
-        lax.fori_loop(0, 16, one, 0)
-
-    @pl.when(y == 1)
-    def _():
-        def note(b, n):
-            order[n] = b
-            return n + (far_any[b, 0] > 0).astype(jnp.int32)
-
-        n = lax.fori_loop(0, 16, note, 0)
-
-        def unseen(b, first):
-            return jnp.where(far_any[b, 0] > 0, first, b)
-
-        order[n] = lax.fori_loop(0, 16, unseen, 0)
-        state = (qs, dos, qt, dot, lseb, delb)
-        for xx in range(NX):
-            load_rows(xx, 1, qg, dog, stg, eye, *state)
-        turn_rows(0, NX, eye, *state[:4])
-        for ref, src in ((dka, dka_in), (dva, dva_in)):
-            ref[...] = src[...]
-        dqa[...] = jnp.zeros_like(dqa)
-
-        def pair(i, carry):
-            tile(
-                (0, 1, 2, 3), order[2 * i], order[2 * i + 1], kvg, far_bias, None,
-                *state, pbuf, dsbuf, dqa, dka, dva,
-            )
-            return carry
-
-        lax.fori_loop(0, (n + 1) // 2, pair, 0)
-        put_dq(dq, dqa)
-        finish(dka, dva)
-
-    @pl.when(y != 1)
-    def _():
-        finish(dka_in, dva_in)
-
-
-def far(far_any, *args):
-    vmem = pl.BlockSpec(memory_space=pltpu.VMEM)
-    return pl.pallas_call(
-        far_kernel,
-        out_shape=(
-            jax.ShapeDtypeStruct((PEERS, TOK, GW), BF16),
-            jax.ShapeDtypeStruct((NZ, 2, NX, PIECE, HD), BF16),
-        ),
-        in_specs=[pl.BlockSpec(memory_space=pltpu.SMEM)] + [vmem] * 7,
-        out_specs=(vmem, vmem),
-        scratch_shapes=[
-            pltpu.SMEM((32,), jnp.int32),
-            *TILE_SCRATCH,
-            pltpu.VMEM((16, HD, BLOCK), F32),
-            pltpu.VMEM((16, HD, BLOCK), F32),
-        ],
-        compiler_params=pltpu.CompilerParams(vmem_limit_bytes=24 << 20),
-        name="far",
-    )(far_any, *args)
-
-
-def give_kernel(
-    dq, far_dq, dkv, gq, gk, gv,
-    land, total, acc_in, acc_out, final,
-    cr_s, cr_r, ring_s, ring_r, q_s, q_r, q_l, kv_s, kv_r, kv_l,
-):
-    y, x, z, core = coords()
-    me = x * 2 + core
-    bar = pltpu.get_barrier_semaphore()
-    signal_peers(bar, y, x, z, core, me)
-    wait_peers(bar, y)
-
-    def cols(ref, g, width):
-        return ref.at[:, pl.ds(pl.multiple_of(g * width, 128), width)]
-
-    def cross_copy(s):
-        return remote(far_dq.at[s], land.at[s], cr_s.at[s], cr_r.at[s], device(3 - y, x, z, core))
-
-    slots = [(me + d) % PEERS for d in (2, 3, 4, 5, 6, 7, 1, 0)]
-
-    @pl.when(y == 1)
-    def _():
-        for s in slots:
-            cross_copy(s).start()
-
-    def ring_copy(direction, piece, steps, step):
-        sign = (1, NZ - 1)[direction]
-        owner = (z + sign * (steps - step)) % NZ
-        if step == 0:
-            src = dkv.at[owner, piece]
-        else:
-            src = acc_out.at[direction, piece, step]
-        return remote(
-            src, acc_in.at[direction, piece, step],
-            ring_s.at[direction, piece, step], ring_r.at[direction, piece, step],
-            device(y, x, (z + sign) % NZ, core),
-        )
-
-    for direction, piece, steps in CHAINS:
-        ring_copy(direction, piece, steps, 0).start()
-
-    def q_copy(src, p):
-        return remote(
-            src.at[p], cols(gq, me, GW), q_s.at[p], q_r.at[me], device(y, p // 2, z, p % 2)
-        )
-
-    def q_recv(s):
-        return remote(
-            total.at[s], cols(gq, s, GW), q_s.at[s], q_r.at[s], device(y, s // 2, z, s % 2)
-        )
-
-    q_local = pltpu.make_async_copy(total.at[me], cols(gq, me, GW), q_l)
-    q_local_direct = pltpu.make_async_copy(dq.at[me], cols(gq, me, GW), q_l)
-
-    @pl.when(y != 2)
-    def _():
-        for p in slots[:-1]:
-            q_copy(dq, p).start()
-        q_local_direct.start()
-
-    def add_cross(some):
-        @pl.when(y == 2)
-        def _():
-            for s in some:
-                cross_copy(s).wait_recv()
-                total[s] = (dq[s].astype(F32) + land[s].astype(F32)).astype(BF16)
-                if s is slots[-1]:
-                    q_local.start()
-                else:
-                    q_copy(total, s).start()
-
-    groups = ((), slots[0:2], slots[2:5], slots[5:8])
-    for step in range(1, 4):
-        for direction, piece, steps in CHAINS:
-            if step < steps:
-                sign = (1, NZ - 1)[direction]
-                owner = (z + sign * (steps - step)) % NZ
-                ring_copy(direction, piece, steps, step - 1).wait_recv()
-                acc_out[direction, piece, step] = (
-                    acc_in[direction, piece, step - 1].astype(F32)
-                    + dkv[owner, piece].astype(F32)
-                ).astype(BF16)
-                ring_copy(direction, piece, steps, step).start()
-        add_cross(groups[step])
-
-    def kv_copy(piece, p):
-        return remote(
-            final.at[piece, p // 2, pl.ds((p % 2) * TOK, TOK), :],
-            cols((gk, gv)[piece], me, HD),
-            kv_s.at[piece, p], kv_r.at[piece, me], device(y, p // 2, z, p % 2),
-        )
-
-    def kv_recv(piece, s):
-        return remote(
-            final.at[piece, s // 2, pl.ds((s % 2) * TOK, TOK), :],
-            cols((gk, gv)[piece], s, HD),
-            kv_s.at[piece, s], kv_r.at[piece, s], device(y, s // 2, z, s % 2),
-        )
-
-    kv_local = []
-    for piece in (0, 1):
-        last = [(d, steps) for d, pc, steps in CHAINS if pc == piece]
-        for direction, steps in last:
-            ring_copy(direction, piece, steps, steps - 1).wait_recv()
-        (d0, s0), (d1, s1) = last
-        final[piece] = (
-            acc_in[d0, piece, s0 - 1].astype(F32)
-            + acc_in[d1, piece, s1 - 1].astype(F32)
-            + dkv[z, piece].astype(F32)
-        ).astype(BF16)
-        for p in slots[:-1]:
-            kv_copy(piece, p).start()
-        local = pltpu.make_async_copy(
-            final.at[piece, x, pl.ds(core * TOK, TOK), :], cols((gk, gv)[piece], me, HD), kv_l.at[piece]
-        )
-        local.start()
-        kv_local.append(local)
-
-    @pl.when(y == 1)
-    def _():
-        for s in slots:
-            cross_copy(s).wait_send()
-
-    for direction, piece, steps in CHAINS:
-        for step in range(steps):
-            ring_copy(direction, piece, steps, step).wait_send()
-    for p in slots[:-1]:
-        q_copy(total, p).wait_send()
-        q_recv(p).wait_recv()
-        for piece in (0, 1):
-            kv_copy(piece, p).wait_send()
-            kv_recv(piece, p).wait_recv()
-    q_local.wait()
-    for c in kv_local:
-        c.wait()
-
-
-def give(dq, far_dq, dkv):
-    vmem = pl.BlockSpec(memory_space=pltpu.VMEM)
-    dma = pltpu.SemaphoreType.DMA
-    return pl.pallas_call(
-        give_kernel,
-        out_shape=(
-            jax.ShapeDtypeStruct((TOK, QH * HD), BF16),
-            jax.ShapeDtypeStruct((TOK, KVH * HD), BF16),
-            jax.ShapeDtypeStruct((TOK, KVH * HD), BF16),
-        ),
-        in_specs=[vmem] * 3,
-        out_specs=(vmem,) * 3,
-        scratch_shapes=[
-            pltpu.VMEM((PEERS, TOK, GW), BF16),
-            pltpu.VMEM((PEERS, TOK, GW), BF16),
-            pltpu.VMEM((2, 2, 4, NX, PIECE, HD), BF16),
-            pltpu.VMEM((2, 2, 4, NX, PIECE, HD), BF16),
-            pltpu.VMEM((2, NX, PIECE, HD), BF16),
             dma((PEERS,)), dma((PEERS,)),
             dma((2, 2, 4)), dma((2, 2, 4)),
             dma((PEERS,)), dma((PEERS,)), dma,
             dma((2, PEERS)), dma((2, PEERS)), dma((2,)),
         ],
-        compiler_params=pltpu.CompilerParams(collective_id=1, has_side_effects=True, vmem_limit_bytes=16 << 20),
-        name="give",
-    )(dq, far_dq, dkv)
+        compiler_params=pltpu.CompilerParams(
+            collective_id=0, has_side_effects=True, vmem_limit_bytes=40 << 20
+        ),
+        name="whole",
+    )(*args)
 
 
 def local(query_act, key_act, value_act, attn_out, grad_out, log_sum, kv_lists):
     args = (query_act, key_act, value_act, attn_out, grad_out, log_sum, kv_lists)
-    qg, dog, stg, kvg, dq, dka, dva, far_bias, far_any = gather(
-        *(pltpu.with_memory_space_constraint(a, pltpu.HBM) for a in args)
-    )
-    far_dq, dkv = far(far_any, qg, dog, stg, kvg, far_bias, dka, dva)
-    return give(dq, far_dq, dkv)
+    return whole(*(pltpu.with_memory_space_constraint(a, pltpu.HBM) for a in args))
 
 
 def solution(mesh):

time: 72.3 us -> 62.6 us (0.87); the launches traced: 72.9 us -> 61.4 us
  Pallas kernels: 70.3 us -> 58.8 us
    pallas_call x3 -> x1, Pallas kernels: 70.3 us -> 58.8 us  [whole(): pl.pallas_call(whole_kernel, out_shape=(jax.ShapeDtypeStruct((TOK, QH * H...]
where the time goes in v2:
time: 62.6 us; the launch traced here: 61.4 us
  Pallas kernels  58.8 us (94%)
  local copies, waits for them, and re-layouts  1.98 us (3%)
  between operations  0.64 us (1%)
    pallas_call x1, Pallas kernels, whole(): pl.pallas_call(whole_kernel, out_shape=(jax.ShapeDtypeStruct((TOK, QH * H...  58.8 us
    unnamed x3, local copies, waits for them, and re-layouts  1.98 us

profile of v2, /device:TPU:9, one launch (start us, length us, event | category | flops | bytes accessed | tf_op | source)
XLA Modules:
  0.0 61.4 jit_solution(14604832333970222903)
XLA Ops:
  0.6 58.8 %whole.1 = (bf16[32,5120]{1,0:T(8,128)(2,1)S(1)}, bf16[32,1024]{1,0:T(8,128)(2,1)S(1)}, bf16[32,1024]{1,0:T(8,128)(2,1)S(1)}) custom-call(bf16[32,5120]{1,0:T(8,128)(2,1)} %q.1, bf16[32,1024]{1,0:T(8,128)(2,1)} %k.1, bf16[32,1024]{1,0:T(8,128)(2,1)} %v.1, bf16[32,5120]{1,0:T(8,128)(2,1)} %o.1, bf16[32,5120]{1,0:T(8,128)(2,1)} %do.1, f32[32,40]{1,0:T(8,128)} %lse.1, ...), custom_call_target="tpu_custom_call" | custom-call | tf_op jit(solution)/shard_map/whole/pallas_call | solution.py:621
  59.5 0.7 %copy.13 = bf16[32,5120]{1,0:T(8,128)(2,1)} copy(bf16[32,5120]{1,0:T(8,128)(2,1)S(1)} %get-tuple-element.6) | data formatting | bytes 655360
  60.2 0.6 %copy.14 = bf16[32,1024]{1,0:T(8,128)(2,1)} copy(bf16[32,1024]{1,0:T(8,128)(2,1)S(1)} %get-tuple-element.7) | data formatting | bytes 131072
  60.8 0.6 %copy.15 = bf16[32,1024]{1,0:T(8,128)(2,1)} copy(bf16[32,1024]{1,0:T(8,128)(2,1)S(1)} %get-tuple-element.8) | data formatting | bytes 131072

commit v3 on v2

--- a/solution.py
+++ b/solution.py
@@ -62,11 +62,14 @@
 
     @pl.when((y == 1) | (y == 2))
     def _():
-        pl.semaphore_signal(bar, inc=1, device_id=device(3 - y, x, z, core), device_id_type=MESH)
+        for p in range(PEERS):
+            pl.semaphore_signal(
+                bar, inc=1, device_id=device(3 - y, p // 2, z, p % 2), device_id_type=MESH
+            )
 
 
 def wait_peers(bar, y):
-    pl.semaphore_wait(bar, PEERS - 1 + 2 + ((y == 1) | (y == 2)).astype(jnp.int32))
+    pl.semaphore_wait(bar, PEERS - 1 + 2 + PEERS * ((y == 1) | (y == 2)).astype(jnp.int32))
 
 
 CHAINS = ((0, 0, 4), (0, 1, 3), (1, 1, 4), (1, 0, 3))
@@ -175,7 +178,7 @@
 def whole_kernel(
     q, k, v, o, do, lse, lists,
     gq, gk, gv,
-    qg, dog, stg, kvg, dq, far_dq, dka, dva, dkv, land, total, acc_in, acc_out, final,
+    qg, dog, stg, kvg, dq, far_dq, dka, dva, dkv, land, acc_in, acc_out, final,
     o_buf, do_buf, lse_buf, rows_buf, stat_src, list_src, lsg, bias, diag,
     qs, dos, qt, dot, lseb, delb, pbuf, dsbuf, dqa, in_sem,
     kv_s, kv_r, kv_l, big_s, big_r, big_l, st_s, st_r, st_l, ls_s, ls_r, ls_l,
@@ -269,6 +272,26 @@
     loads[0].wait()
     list_src[...] = jnp.full((8, 128), -1, jnp.int32)
     list_src[0:2, 0:LISTW] = rows_buf[...]
+
+    wait_peers(bar, y)
+    for piece in (0, 1):
+        for n in NEAR[1:] + NEAR[:1]:
+            kv_copy(to(n), piece).start()
+    for n in NEAR[:5]:
+        for which in (0, 1):
+            big_copy(to(n), which).start()
+    for c in big_local:
+        c.wait()
+
+    @pl.when(y == 2)
+    def _():
+        for which in (0, 1):
+            cross_copy(me, which).start()
+
+    for d in range(1, NX):
+        ls_copy(d).start()
+    ls_local = pltpu.make_async_copy(list_src, lsg.at[0, x], ls_l)
+    ls_local.start()
 
     for c in loads[1:]:
         c.wait()
@@ -285,6 +308,60 @@
             block = jnp.where(lane == 8 + r, delta, block)
         stat_src[g] = block
 
+    for n in NEAR:
+        st_copy(to(n)).start()
+    st_local = pltpu.make_async_copy(stat_src.at[me], stg.at[0, me], st_l)
+    st_local.start()
+    for n in NEAR[5:]:
+        for which in (0, 1):
+            big_copy(to(n), which).start()
+
+    def ring_copy(direction, piece, step):
+        sign = (1, NZ - 1)[direction]
+        back = (NZ - 1, 1)[direction]
+        chunk = (z + back * step) % NZ
+        part = kvg.at[chunk, piece]
+        return remote(
+            part, part, ring_s.at[direction, piece, step], ring_r.at[direction, piece, step],
+            device(y, x, (z + sign) % NZ, core),
+        )
+
+    def ring_recv(direction, piece, step):
+        back = (NZ - 1, 1)[direction]
+        chunk = (z + back * (step + 1)) % NZ
+        part = kvg.at[chunk, piece]
+        return remote(
+            part, part, ring_s.at[direction, piece, step], ring_r.at[direction, piece, step],
+            device(y, x, (z + back) % NZ, core),
+        )
+
+    def forward(some):
+        for n in some:
+            s = of(n)
+            for which in (0, 1):
+                big_recv(s, which).wait_recv()
+
+            @pl.when(y == 2)
+            def _():
+                for which in (0, 1):
+                    cross_copy(s, which).start()
+
+    def ring_start(piece):
+        for n in NEAR:
+            kv_recv(of(n), piece).wait_recv()
+        kv_local[piece].wait()
+        for direction in (0, 1):
+            ring_copy(direction, piece, 0).start()
+
+    def ring_step(step, piece):
+        for direction, pc, steps in CHAINS:
+            if pc == piece and step < steps:
+                ring_recv(direction, piece, step).wait_recv()
+                if step + 1 < steps:
+                    ring_copy(direction, piece, step + 1).start()
+
+    ring_start(0)
+    ring_start(1)
     for ref in (dka, dva, dqa):
         ref[...] = jnp.zeros_like(ref)
     eye = identity()
@@ -295,76 +372,6 @@
     diag[0] = jnp.where(key_tok <= row_tok, 0.0, BIG)
     diag[1] = jnp.zeros((ROWS, 128), F32)
 
-    wait_peers(bar, y)
-    for piece in (0, 1):
-        for n in NEAR[1:] + NEAR[:1]:
-            kv_copy(to(n), piece).start()
-    for n in NEAR:
-        for which in (0, 1):
-            big_copy(to(n), which).start()
-    for c in big_local:
-        c.wait()
-
-    @pl.when(y == 2)
-    def _():
-        for which in (0, 1):
-            cross_copy(me, which).start()
-
-    for n in NEAR:
-        st_copy(to(n)).start()
-    for d in range(1, NX):
-        ls_copy(d).start()
-    st_local = pltpu.make_async_copy(stat_src.at[me], stg.at[0, me], st_l)
-    st_local.start()
-    ls_local = pltpu.make_async_copy(list_src, lsg.at[0, x], ls_l)
-    ls_local.start()
-
-    def ring_copy(direction, piece, step):
-        sign = (1, NZ - 1)[direction]
-        back = (NZ - 1, 1)[direction]
-        chunk = (z + back * step) % NZ
-        part = kvg.at[chunk, piece]
-        return remote(
-            part, part, ring_s.at[direction, piece, step], ring_r.at[direction, piece, step],
-            device(y, x, (z + sign) % NZ, core),
-        )
-
-    def ring_recv(direction, piece, step):
-        back = (NZ - 1, 1)[direction]
-        chunk = (z + back * (step + 1)) % NZ
-        part = kvg.at[chunk, piece]
-        return remote(
-            part, part, ring_s.at[direction, piece, step], ring_r.at[direction, piece, step],
-            device(y, x, (z + back) % NZ, core),
-        )
-
-    def forward(some):
-        for n in some:
-            s = of(n)
-            for which in (0, 1):
-                big_recv(s, which).wait_recv()
-
-            @pl.when(y == 2)
-            def _():
-                for which in (0, 1):
-                    cross_copy(s, which).start()
-
-    def ring_start(piece):
-        for n in NEAR:
-            kv_recv(of(n), piece).wait_recv()
-        kv_local[piece].wait()
-        for direction in (0, 1):
-            ring_copy(direction, piece, 0).start()
-
-    def ring_step(step, piece):
-        for direction, pc, steps in CHAINS:
-            if pc == piece and step < steps:
-                ring_recv(direction, piece, step).wait_recv()
-                if step + 1 < steps:
-                    ring_copy(direction, piece, step + 1).start()
-
-    ring_start(0)
-    ring_start(1)
     forward(NEAR[:3])
     ring_step(0, 0)
     forward(NEAR[3:4])
@@ -420,21 +427,21 @@
     put_dq(dq, dqa)
 
     def cross_dq(s):
-        return remote(far_dq.at[s], land.at[s], dq_s.at[s], dq_r.at[s], device(3 - y, x, z, core))
-
-    def dq_copy(src, p):
-        return remote(src.at[p], cols(gq, me, GW), out_s.at[p], out_r.at[me], at(p))
+        return remote(far_dq.at[s], land.at[me], dq_s.at[s], dq_r.at[me], device(3 - y, s // 2, z, s % 2))
+
+    def cross_dq_recv(s):
+        return remote(far_dq.at[s], land.at[s], dq_s.at[s], dq_r.at[s], device(3 - y, s // 2, z, s % 2))
+
+    def dq_copy(p):
+        return remote(dq.at[p], cols(gq, me, GW), out_s.at[p], out_r.at[me], at(p))
 
     def dq_recv(s):
-        return remote(total.at[s], cols(gq, s, GW), out_s.at[s], out_r.at[s], at(s))
-
-    dq_local = pltpu.make_async_copy(total.at[me], cols(gq, me, GW), out_l)
-
-    @pl.when(y != 2)
-    def _():
-        for n in NEAR:
-            dq_copy(dq, to(n)).start()
-        pltpu.make_async_copy(dq.at[me], cols(gq, me, GW), out_l).start()
+        return remote(dq.at[s], cols(gq, s, GW), out_s.at[s], out_r.at[s], at(s))
+
+    dq_local = pltpu.make_async_copy(dq.at[me], cols(gq, me, GW), out_l)
+    for n in NEAR:
+        dq_copy(to(n)).start()
+    dq_local.start()
 
     @pl.when(y == 1)
     def _():
@@ -471,19 +478,25 @@
         ).astype(BF16)
         red_copy(direction, piece, steps, step).start()
 
+    def turn_column(zz):
+        for xx in range(NX):
+            for piece, ref, scale in ((0, dka, SCALE), (1, dva, 1.0)):
+                low = (ref[zz + 4 * xx] * scale).astype(BF16)
+                turned = lax.dot_general(eye, low, NT, preferred_element_type=F32).astype(BF16)
+                dkv[2 * zz, piece, xx] = turned[:PIECE]
+                dkv[2 * zz + 1, piece, xx] = turned[PIECE:]
+
     def finish(zz):
         @pl.when(y == 1)
         def _():
             rest = (pbuf, dsbuf, dqa, dka, dva)
             tile((0, 1, 2, 3), zz, zz + 4, kvg, bias, None, *state, *rest)
             tile((0, 1, 2, 3), zz + 8, zz + 12, kvg, bias, None, *state, *rest)
-
-        for xx in range(NX):
-            for piece, ref, scale in ((0, dka, SCALE), (1, dva, 1.0)):
-                low = (ref[zz + 4 * xx] * scale).astype(BF16)
-                turned = lax.dot_general(eye, low, NT, preferred_element_type=F32).astype(BF16)
-                dkv[2 * zz, piece, xx] = turned[:PIECE]
-                dkv[2 * zz + 1, piece, xx] = turned[PIECE:]
+            turn_column(zz)
+
+        @pl.when(y != 1)
+        def _():
+            turn_column(zz)
 
     long = ((0, 0, 4), (1, 1, 4))
     short = ((0, 1, 3), (1, 0, 3))
@@ -560,21 +573,6 @@
         )
         grad_local[piece].start()
 
-    @pl.when(y == 2)
-    def _():
-        for s in range(PEERS):
-            cross_dq(s).wait_recv()
-            total[s] = (dq[s].astype(F32) + land[s].astype(F32)).astype(BF16)
-
-            @pl.when(s == me)
-            def _():
-                dq_local.start()
-
-            @pl.when(s != me)
-            def _():
-                dq_copy(total, s).start()
-
-
     for n in NEAR:
         for i in (0, 1):
             kv_copy(to(n), i).wait_send()
@@ -607,11 +605,18 @@
         for piece in (0, 1):
             grad_copy(piece, to(n)).wait_send()
             grad_recv(piece, of(n)).wait_recv()
-        dq_copy(total, to(n)).wait_send()
+        dq_copy(to(n)).wait_send()
         dq_recv(of(n)).wait_recv()
     for c in grad_local:
         c.wait()
     dq_local.wait()
+
+    @pl.when(y == 2)
+    def _():
+        for g in range(PEERS):
+            cross_dq_recv(g).wait_recv()
+            own_cols = slice(g * GW, (g + 1) * GW)
+            gq[:, own_cols] = (gq[:, own_cols].astype(F32) + land[g].astype(F32)).astype(BF16)
 
 
 def whole(*args):
@@ -637,7 +642,6 @@
             pltpu.VMEM((16, HD, BLOCK), F32),
             pltpu.VMEM((16, HD, BLOCK), F32),
             pltpu.VMEM((NZ, 2, NX, PIECE, HD), BF16),
-            pltpu.VMEM((PEERS, TOK, GW), BF16),
             pltpu.VMEM((PEERS, TOK, GW), BF16),
             pltpu.VMEM((2, 2, 4, NX, PIECE, HD), BF16),
             pltpu.VMEM((2, 2, 4, NX, PIECE, HD), BF16),
@@ -672,9 +676,31 @@
     )(*args)
 
 
+def emit_kernel(a, b, c, x, y, z, sem):
+    copies = [
+        pltpu.make_async_copy(src, dst, sem.at[i]) for i, (src, dst) in enumerate(((a, x), (b, y), (c, z)))
+    ]
+    for one in copies:
+        one.start()
+    for one in copies:
+        one.wait()
+
+
+def emit(*arrays):
+    return pl.pallas_call(
+        emit_kernel,
+        out_shape=tuple(jax.ShapeDtypeStruct(a.shape, a.dtype) for a in arrays),
+        in_specs=[pl.BlockSpec(memory_space=pltpu.VMEM)] * 3,
+        out_specs=(pl.BlockSpec(memory_space=pltpu.HBM),) * 3,
+        scratch_shapes=[pltpu.SemaphoreType.DMA((3,))],
+        compiler_params=pltpu.CompilerParams(vmem_limit_bytes=1 << 20),
+        name="emit",
+    )(*arrays)
+
+
 def local(query_act, key_act, value_act, attn_out, grad_out, log_sum, kv_lists):
     args = (query_act, key_act, value_act, attn_out, grad_out, log_sum, kv_lists)
-    return whole(*(pltpu.with_memory_space_constraint(a, pltpu.HBM) for a in args))
+    return emit(*whole(*(pltpu.with_memory_space_constraint(a, pltpu.HBM) for a in args)))
 
 
 def solution(mesh):

time: 62.6 us -> 60.6 us (0.968); the launches traced: 61.4 us -> 60.5 us
  local copies, waits for them, and re-layouts: 1.98 us -> 0 us
  Pallas kernels: 58.8 us -> 59.9 us
    unnamed x3 -> x0, local copies, waits for them, and re-layouts: 1.98 us -> none
    pallas_call x0 -> x1, Pallas kernels: none -> 0.79 us  [emit(): pl.pallas_call(emit_kernel, out_shape=tuple((jax.ShapeDtypeStruct(a.shape...]
where the time goes in v3:
time: 60.6 us; the launch traced here: 60.5 us
  Pallas kernels  59.9 us (99%)
  between operations  0.64 us (1%)
    pallas_call x1, Pallas kernels, whole(): pl.pallas_call(whole_kernel, out_shape=(jax.ShapeDtypeStruct((TOK, QH * H...  59.1 us

profile of v3, /device:TPU:9, one launch (start us, length us, event | category | flops | bytes accessed | tf_op | source)
XLA Modules:
  0.0 60.5 jit_solution(4955406187804079795)
XLA Ops:
  0.6 59.1 %whole.1 = (bf16[32,5120]{1,0:T(8,128)(2,1)S(1)}, bf16[32,1024]{1,0:T(8,128)(2,1)S(1)}, bf16[32,1024]{1,0:T(8,128)(2,1)S(1)}) custom-call(bf16[32,5120]{1,0:T(8,128)(2,1)} %q.1, bf16[32,1024]{1,0:T(8,128)(2,1)} %k.1, bf16[32,1024]{1,0:T(8,128)(2,1)} %v.1, bf16[32,5120]{1,0:T(8,128)(2,1)} %o.1, bf16[32,5120]{1,0:T(8,128)(2,1)} %do.1, f32[32,40]{1,0:T(8,128)} %lse.1, ...), custom_call_target="tpu_custom_call" | custom-call | tf_op jit(solution)/shard_map/whole/pallas_call | solution.py:626
  59.7 0.8 %emit.1 = (bf16[32,5120]{1,0:T(8,128)(2,1)}, bf16[32,1024]{1,0:T(8,128)(2,1)}, bf16[32,1024]{1,0:T(8,128)(2,1)}) custom-call(bf16[32,5120]{1,0:T(8,128)(2,1)S(1)} %get-tuple-element.6.a, bf16[32,1024]{1,0:T(8,128)(2,1)S(1)} %get-tuple-element.7.b, bf16[32,1024]{1,0:T(8,128)(2,1)S(1)} %get-tuple-element.8.c), custom_call_target="tpu_custom_call" | custom-call | tf_op jit(solution)/shard_map/emit/pallas_call | solution.py:690

commit v4 on v3

--- a/solution.py
+++ b/solution.py
@@ -120,9 +120,10 @@
     return jnp.concatenate([kvg[zz, piece, b // 4], kvg[zz + 1, piece, b // 4]], axis=0)
 
 
-def tile(xs, a, b, kvg, bias, diag, qs, dos, qt, dot, lseb, delb, pbuf, dsbuf, dqa, dka, dva):
+def tile(xs, a, b, kvg, bias, diag, eye, qs, dos, qt, dot, lseb, delb, pbuf, dsbuf, dqa, dka, dva):
     keys = jnp.concatenate([key_block(kvg, 0, a), key_block(kvg, 0, b)], axis=0)
     values = jnp.concatenate([key_block(kvg, 1, a), key_block(kvg, 1, b)], axis=0)
+    turned = lax.dot_general(eye, keys, NT, preferred_element_type=F32).astype(BF16)
     for x in xs:
         at = rows_of(x)
         s = lax.dot_general(qs[at, :], keys, NT, preferred_element_type=F32)
@@ -139,24 +140,24 @@
         ds = (p * (dp - jnp.concatenate([delta, delta], axis=1))).astype(BF16)
         pbuf[at, :] = p.astype(BF16)
         dsbuf[at, :] = ds
-        dqa[at, :] += lax.dot_general(ds, keys, NN, preferred_element_type=F32)
     at = slice(xs[0] * ROWS, (xs[-1] + 1) * ROWS)
     dvt = lax.dot_general(dot[:, at], pbuf[at, :], NN, preferred_element_type=F32)
     dkt = lax.dot_general(qt[:, at], dsbuf[at, :], NN, preferred_element_type=F32)
+    dqa[:, at] += lax.dot_general(turned, dsbuf[at, :], NT, preferred_element_type=F32)
     dva[a] += dvt[:, :BLOCK]
     dka[a] += dkt[:, :BLOCK]
     dva[b] += dvt[:, BLOCK:]
     dka[b] += dkt[:, BLOCK:]
 
 
-def put_dq(dq, dqa):
-    for x in range(NX):
-        for c in range(2):
-            for r in range(GS):
-                start = x * ROWS + r * PIECE + c * TOK
-                dq[x * 2 + c, :, r * HD : (r + 1) * HD] = (
-                    dqa[start : start + TOK, :] * SCALE
-                ).astype(BF16)
+def put_dq(dq, dqa, eye):
+    for j in range(ALLROWS // 128):
+        low = (dqa[:, j * 128 : (j + 1) * 128] * SCALE).astype(BF16)
+        rows = lax.dot_general(eye, low, NT, preferred_element_type=F32).astype(BF16)
+        for i in range(128 // TOK):
+            x, rest = divmod(j * 4 + i, 2 * GS)
+            r, c = divmod(rest, 2)
+            dq[x * 2 + c, :, r * HD : (r + 1) * HD] = rows[i * TOK : (i + 1) * TOK]
 
 
 TILE_SCRATCH = [
@@ -166,9 +167,9 @@
     pltpu.VMEM((HD, ALLROWS), BF16),
     pltpu.VMEM((ALLROWS, 128), F32),
     pltpu.VMEM((ALLROWS, 128), F32),
-    pltpu.VMEM((ALLROWS, 2 * BLOCK), BF16),
-    pltpu.VMEM((ALLROWS, 2 * BLOCK), BF16),
-    pltpu.VMEM((ALLROWS, HD), F32),
+    pltpu.VMEM((2, ALLROWS, 2 * BLOCK), BF16),
+    pltpu.VMEM((2, ALLROWS, 2 * BLOCK), BF16),
+    pltpu.VMEM((HD, ALLROWS), F32),
 ]
 
 
@@ -418,13 +419,13 @@
         move = jnp.where(i == 1, side, jnp.where(i == 2, -side, jnp.where(i == 3, 2, 0)))
         zz = (own + move + 4) % 4
         cut = diag.at[jnp.where(i == 0, 0, 1)]
-        rest = (pbuf, dsbuf, dqa, dka, dva)
-        tile((0, 1, 2, 3), zz, zz + 4, kvg, bias, cut, *state, *rest)
-        tile((2, 3), zz + 8, zz + 12, kvg, bias, cut, *state, *rest)
+        rest = [(pbuf.at[n], dsbuf.at[n], dqa, dka, dva) for n in (0, 1)]
+        tile((0, 1, 2, 3), zz, zz + 4, kvg, bias, cut, eye, *state, *rest[0])
+        tile((2, 3), zz + 8, zz + 12, kvg, bias, cut, eye, *state, *rest[1])
         return carry
 
     lax.fori_loop(0, 4, column, 0)
-    put_dq(dq, dqa)
+    put_dq(dq, dqa, eye)
 
     def cross_dq(s):
         return remote(far_dq.at[s], land.at[me], dq_s.at[s], dq_r.at[me], device(3 - y, s // 2, z, s % 2))
@@ -489,9 +490,9 @@
     def finish(zz):
         @pl.when(y == 1)
         def _():
-            rest = (pbuf, dsbuf, dqa, dka, dva)
-            tile((0, 1, 2, 3), zz, zz + 4, kvg, bias, None, *state, *rest)
-            tile((0, 1, 2, 3), zz + 8, zz + 12, kvg, bias, None, *state, *rest)
+            rest = [(pbuf.at[n], dsbuf.at[n], dqa, dka, dva) for n in (0, 1)]
+            tile((0, 1, 2, 3), zz, zz + 4, kvg, bias, None, eye, *state, *rest[0])
+            tile((0, 1, 2, 3), zz + 8, zz + 12, kvg, bias, None, eye, *state, *rest[1])
             turn_column(zz)
 
         @pl.when(y != 1)
@@ -530,7 +531,7 @@
 
     @pl.when(y == 1)
     def _():
-        put_dq(far_dq, dqa)
+        put_dq(far_dq, dqa, eye)
         for s in range(PEERS):
             cross_dq(s).start()
 

time: 60.6 us -> 57.9 us (0.955)
  Pallas kernels: 59.9 us -> 57.2 us
    pallas_call x1, Pallas kernels: 59.1 us -> 56.4 us  [whole(): pl.pallas_call(whole_kernel, out_shape=(jax.ShapeDtypeStruct((TOK, QH * H...]
where the time goes in v4:
time: 57.9 us; the launch traced here: 57.8 us
  Pallas kernels  57.2 us (99%)
  between operations  0.64 us (1%)
    pallas_call x1, Pallas kernels, whole(): pl.pallas_call(whole_kernel, out_shape=(jax.ShapeDtypeStruct((TOK, QH * H...  56.4 us

profile of v4, /device:TPU:9, one launch (start us, length us, event | category | flops | bytes accessed | tf_op | source)
XLA Modules:
  0.0 57.8 jit_solution(14170602259754525252)
XLA Ops:
  0.6 56.4 %whole.1 = (bf16[32,5120]{1,0:T(8,128)(2,1)S(1)}, bf16[32,1024]{1,0:T(8,128)(2,1)S(1)}, bf16[32,1024]{1,0:T(8,128)(2,1)S(1)}) custom-call(bf16[32,5120]{1,0:T(8,128)(2,1)} %q.1, bf16[32,1024]{1,0:T(8,128)(2,1)} %k.1, bf16[32,1024]{1,0:T(8,128)(2,1)} %v.1, bf16[32,5120]{1,0:T(8,128)(2,1)} %o.1, bf16[32,5120]{1,0:T(8,128)(2,1)} %do.1, f32[32,40]{1,0:T(8,128)} %lse.1, ...), custom_call_target="tpu_custom_call" | custom-call | tf_op jit(solution)/shard_map/whole/pallas_call | solution.py:627
  57.0 0.8 %emit.1 = (bf16[32,5120]{1,0:T(8,128)(2,1)}, bf16[32,1024]{1,0:T(8,128)(2,1)}, bf16[32,1024]{1,0:T(8,128)(2,1)}) custom-call(bf16[32,5120]{1,0:T(8,128)(2,1)S(1)} %get-tuple-element.6.a, bf16[32,1024]{1,0:T(8,128)(2,1)S(1)} %get-tuple-element.7.b, bf16[32,1024]{1,0:T(8,128)(2,1)S(1)} %get-tuple-element.8.c), custom_call_target="tpu_custom_call" | custom-call | tf_op jit(solution)/shard_map/emit/pallas_call | solution.py:691

commit v5 on v4

--- a/solution.py
+++ b/solution.py
@@ -169,7 +169,7 @@
     pltpu.VMEM((ALLROWS, 128), F32),
     pltpu.VMEM((2, ALLROWS, 2 * BLOCK), BF16),
     pltpu.VMEM((2, ALLROWS, 2 * BLOCK), BF16),
-    pltpu.VMEM((HD, ALLROWS), F32),
+    pltpu.VMEM((2, HD, ALLROWS), F32),
 ]
 
 
@@ -270,10 +270,6 @@
     for c in kv_local + big_local:
         c.start()
 
-    loads[0].wait()
-    list_src[...] = jnp.full((8, 128), -1, jnp.int32)
-    list_src[0:2, 0:LISTW] = rows_buf[...]
-
     wait_peers(bar, y)
     for piece in (0, 1):
         for n in NEAR[1:] + NEAR[:1]:
@@ -288,6 +284,10 @@
     def _():
         for which in (0, 1):
             cross_copy(me, which).start()
+
+    loads[0].wait()
+    list_src[...] = jnp.full((8, 128), -1, jnp.int32)
+    list_src[0:2, 0:LISTW] = rows_buf[...]
 
     for d in range(1, NX):
         ls_copy(d).start()
@@ -370,8 +370,7 @@
     base = y * 16
     row_tok = (z % 2) * PIECE + lax.broadcasted_iota(jnp.int32, (ROWS, 128), 0) % PIECE
     key_tok = lax.broadcasted_iota(jnp.int32, (ROWS, 128), 1)
-    diag[0] = jnp.where(key_tok <= row_tok, 0.0, BIG)
-    diag[1] = jnp.zeros((ROWS, 128), F32)
+    diag[...] = jnp.where(key_tok <= row_tok, 0.0, BIG)
 
     forward(NEAR[:3])
     ring_step(0, 0)
@@ -403,12 +402,23 @@
         for i in (0, 1):
             load_rows(piece * 2 + i, 0, qg, dog, stg, eye, *state)
         turn_rows(piece * 2, piece * 2 + 2, eye, *state[:4])
-        ring_step(2, piece)
     for xx in range(NX):
         bias[xx] = jnp.where(seen_bias(lsg, 0, xx, half, base) > 0.0, 0.0, BIG)
 
     own = z // 2
     side = (z % 2) * 2 - 1
+
+    def own_tiles(zz, cut, between):
+        rest = [(pbuf.at[n], dsbuf.at[n], dqa.at[0], dka, dva) for n in (0, 1)]
+        tile((0, 1, 2, 3), zz, zz + 4, kvg, bias, cut, eye, *state, *rest[0])
+        between()
+        tile((2, 3), zz + 8, zz + 12, kvg, bias, cut, eye, *state, *rest[1])
+
+    def third_hop():
+        ring_step(2, 0)
+        ring_step(2, 1)
+
+    own_tiles(own, diag, third_hop)
 
     def column(i, carry):
         @pl.when(i == 3)
@@ -416,16 +426,11 @@
             ring_step(3, 0)
             ring_step(3, 1)
 
-        move = jnp.where(i == 1, side, jnp.where(i == 2, -side, jnp.where(i == 3, 2, 0)))
-        zz = (own + move + 4) % 4
-        cut = diag.at[jnp.where(i == 0, 0, 1)]
-        rest = [(pbuf.at[n], dsbuf.at[n], dqa, dka, dva) for n in (0, 1)]
-        tile((0, 1, 2, 3), zz, zz + 4, kvg, bias, cut, eye, *state, *rest[0])
-        tile((2, 3), zz + 8, zz + 12, kvg, bias, cut, eye, *state, *rest[1])
+        move = jnp.where(i == 1, side, jnp.where(i == 2, -side, 2))
+        own_tiles((own + move + 4) % 4, None, lambda: None)
         return carry
 
-    lax.fori_loop(0, 4, column, 0)
-    put_dq(dq, dqa, eye)
+    lax.fori_loop(1, 4, column, 0)
 
     def cross_dq(s):
         return remote(far_dq.at[s], land.at[me], dq_s.at[s], dq_r.at[me], device(3 - y, s // 2, z, s % 2))
@@ -440,9 +445,14 @@
         return remote(dq.at[s], cols(gq, s, GW), out_s.at[s], out_r.at[s], at(s))
 
     dq_local = pltpu.make_async_copy(dq.at[me], cols(gq, me, GW), out_l)
-    for n in NEAR:
-        dq_copy(to(n)).start()
-    dq_local.start()
+
+    def send_dq():
+        put_dq(dq, dqa.at[0], eye)
+        for n in NEAR:
+            dq_copy(to(n)).start()
+        dq_local.start()
+
+    send_dq()
 
     @pl.when(y == 1)
     def _():
@@ -455,7 +465,6 @@
             load_rows(xx, 1, qg, dog, stg, eye, *state)
             bias[xx] = jnp.where(seen_bias(lsg, 1, xx, half, base) > 0.0, 0.0, BIG)
         turn_rows(0, NX, eye, *state[:4])
-        dqa[...] = jnp.zeros_like(dqa)
 
     def red_copy(direction, piece, steps, step):
         sign = (1, NZ - 1)[direction]
@@ -490,7 +499,7 @@
     def finish(zz):
         @pl.when(y == 1)
         def _():
-            rest = [(pbuf.at[n], dsbuf.at[n], dqa, dka, dva) for n in (0, 1)]
+            rest = [(pbuf.at[n], dsbuf.at[n], dqa.at[1], dka, dva) for n in (0, 1)]
             tile((0, 1, 2, 3), zz, zz + 4, kvg, bias, None, eye, *state, *rest[0])
             tile((0, 1, 2, 3), zz + 8, zz + 12, kvg, bias, None, eye, *state, *rest[1])
             turn_column(zz)
@@ -529,16 +538,16 @@
 
     lax.fori_loop(0, 4, reduce_column, 0)
 
-    @pl.when(y == 1)
-    def _():
-        put_dq(far_dq, dqa, eye)
-        for s in range(PEERS):
-            cross_dq(s).start()
-
     for c in short:
         red_step(*c, 2)
     for c in long:
         red_step(*c, 3)
+
+    @pl.when(y == 1)
+    def _():
+        put_dq(far_dq, dqa.at[1], eye)
+        for s in range(PEERS):
+            cross_dq(s).start()
 
     def grad_copy(piece, p):
         return remote(
@@ -655,7 +664,7 @@
             pltpu.VMEM((8, 128), jnp.int32),
             pltpu.VMEM((2, NX, 8, 128), jnp.int32),
             pltpu.VMEM((NX, 16, 128), F32),
-            pltpu.VMEM((2, ROWS, 128), F32),
+            pltpu.VMEM((ROWS, 128), F32),
             *TILE_SCRATCH,
             dma((4,)),
             dma((2, PEERS)), dma((2, PEERS)), dma((2,)),

time: 57.9 us -> 57.2 us (0.988)
  Pallas kernels: 57.2 us -> 56.5 us
    pallas_call x1, Pallas kernels: 56.4 us -> 55.7 us  [whole(): pl.pallas_call(whole_kernel, out_shape=(jax.ShapeDtypeStruct((TOK, QH * H...]
where the time goes in v5:
time: 57.2 us
  Pallas kernels  56.5 us (99%)
  between operations  0.64 us (1%)
    pallas_call x1, Pallas kernels, whole(): pl.pallas_call(whole_kernel, out_shape=(jax.ShapeDtypeStruct((TOK, QH * H...  55.7 us

profile of v5, /device:TPU:9, one launch (start us, length us, event | category | flops | bytes accessed | tf_op | source)
XLA Modules:
  0.0 57.2 jit_solution(17213183654237333483)
XLA Ops:
  0.6 55.7 %whole.1 = (bf16[32,5120]{1,0:T(8,128)(2,1)S(1)}, bf16[32,1024]{1,0:T(8,128)(2,1)S(1)}, bf16[32,1024]{1,0:T(8,128)(2,1)S(1)}) custom-call(bf16[32,5120]{1,0:T(8,128)(2,1)} %q.1, bf16[32,1024]{1,0:T(8,128)(2,1)} %k.1, bf16[32,1024]{1,0:T(8,128)(2,1)} %v.1, bf16[32,5120]{1,0:T(8,128)(2,1)} %o.1, bf16[32,5120]{1,0:T(8,128)(2,1)} %do.1, f32[32,40]{1,0:T(8,128)} %lse.1, ...), custom_call_target="tpu_custom_call" | custom-call | tf_op jit(solution)/shard_map/whole/pallas_call | solution.py:636
  56.4 0.8 %emit.1 = (bf16[32,5120]{1,0:T(8,128)(2,1)}, bf16[32,1024]{1,0:T(8,128)(2,1)}, bf16[32,1024]{1,0:T(8,128)(2,1)}) custom-call(bf16[32,5120]{1,0:T(8,128)(2,1)S(1)} %get-tuple-element.6.a, bf16[32,1024]{1,0:T(8,128)(2,1)S(1)} %get-tuple-element.7.b, bf16[32,1024]{1,0:T(8,128)(2,1)S(1)} %get-tuple-element.8.c), custom_call_target="tpu_custom_call" | custom-call | tf_op jit(solution)/shard_map/emit/pallas_call | solution.py:700

commit v6 on v5

--- a/solution.py
+++ b/solution.py
@@ -361,8 +361,10 @@
                 if step + 1 < steps:
                     ring_copy(direction, piece, step + 1).start()
 
+    forward(NEAR[:1])
     ring_start(0)
     ring_start(1)
+    forward(NEAR[1:3])
     for ref in (dka, dva, dqa):
         ref[...] = jnp.zeros_like(ref)
     eye = identity()
@@ -372,7 +374,6 @@
     key_tok = lax.broadcasted_iota(jnp.int32, (ROWS, 128), 1)
     diag[...] = jnp.where(key_tok <= row_tok, 0.0, BIG)
 
-    forward(NEAR[:3])
     ring_step(0, 0)
     forward(NEAR[3:4])
     ring_step(0, 1)

time: 57.2 us -> 56.6 us (0.990)
  Pallas kernels: 56.5 us -> 55.9 us
    pallas_call x1, Pallas kernels: 55.7 us -> 55.1 us  [whole(): pl.pallas_call(whole_kernel, out_shape=(jax.ShapeDtypeStruct((TOK, QH * H...]
where the time goes in v6:
time: 56.6 us; the launch traced here: 56.5 us
  Pallas kernels  55.9 us (99%)
  between operations  0.64 us (1%)
    pallas_call x1, Pallas kernels, whole(): pl.pallas_call(whole_kernel, out_shape=(jax.ShapeDtypeStruct((TOK, QH * H...  55.1 us

profile of v6, /device:TPU:9, one launch (start us, length us, event | category | flops | bytes accessed | tf_op | source)
XLA Modules:
  0.0 56.5 jit_solution(8449021494673637615)
XLA Ops:
  0.6 55.1 %whole.1 = (bf16[32,5120]{1,0:T(8,128)(2,1)S(1)}, bf16[32,1024]{1,0:T(8,128)(2,1)S(1)}, bf16[32,1024]{1,0:T(8,128)(2,1)S(1)}) custom-call(bf16[32,5120]{1,0:T(8,128)(2,1)} %q.1, bf16[32,1024]{1,0:T(8,128)(2,1)} %k.1, bf16[32,1024]{1,0:T(8,128)(2,1)} %v.1, bf16[32,5120]{1,0:T(8,128)(2,1)} %o.1, bf16[32,5120]{1,0:T(8,128)(2,1)} %do.1, f32[32,40]{1,0:T(8,128)} %lse.1, ...), custom_call_target="tpu_custom_call" | custom-call | tf_op jit(solution)/shard_map/whole/pallas_call | solution.py:637
  55.8 0.8 %emit.1 = (bf16[32,5120]{1,0:T(8,128)(2,1)}, bf16[32,1024]{1,0:T(8,128)(2,1)}, bf16[32,1024]{1,0:T(8,128)(2,1)}) custom-call(bf16[32,5120]{1,0:T(8,128)(2,1)S(1)} %get-tuple-element.6.a, bf16[32,1024]{1,0:T(8,128)(2,1)S(1)} %get-tuple-element.7.b, bf16[32,1024]{1,0:T(8,128)(2,1)S(1)} %get-tuple-element.8.c), custom_call_target="tpu_custom_call" | custom-call | tf_op jit(solution)/shard_map/emit/pallas_call | solution.py:701
